TPU v7x, 256 devices: a whole 4x4x8 slice. The times are simulated.
256 devices in a mesh: dp: 32 (over y, x, core), ctx: 8 (over z).
Axes of the slice: x: 4, y: 4, z: 8, core: 2. Of those that a mesh axis runs over, the one named last changes fastest.
Arguments:
- value: bfloat16 [32, 1024, 512], P('dp', 'ctx'), may hold values from -6 to 6
- gate_one: bfloat16 [32, 1024, 512], P('dp', 'ctx'), may hold values from -6 to 6
- gate_two: bfloat16 [32, 1024, 512], P('dp', 'ctx'), may hold values from -6 to 6
- filters: bfloat16 [2, 1024, 512], replicated, may hold values from -0.1875 to 0.1875
- out_weight: bfloat16 [512, 512], replicated, may hold values from -0.25 to 0.25
- grad_out: bfloat16 [32, 1024, 512], P('dp', 'ctx'), may hold values from -6 to 6
Outputs:
- mixed: bfloat16 [32, 1024, 512], P('dp', 'ctx')
- grad_value: bfloat16 [32, 1024, 512], P('dp', 'ctx')
- grad_gate_one: bfloat16 [32, 1024, 512], P('dp', 'ctx')
- grad_gate_two: bfloat16 [32, 1024, 512], P('dp', 'ctx')
- filter_grad: float32 [2, 1024, 512], P(None, 'ctx', 'dp')
- weight_grad: float32 [512, 512], P('dp', 'ctx')
All inputs are finite; a program needn't handle non-finite values.
Results may differ from a plain program's by a relative error of at most 0.019.
Values may be sent and summed in bfloat16 or wider, within the bound.
A program may use at most 128 MiB of HBM per device.

v0:
```python
import math

import jax
import jax.numpy as jnp
from jax import lax
from jax.sharding import PartitionSpec as P


def make_tables(block):
    period = 2 * block
    freq_bins = jnp.concatenate(
        [jnp.arange(block + 1, dtype=jnp.int32), jnp.arange(1, block, dtype=jnp.int32)]
    )
    sine_rows = jnp.arange(period, dtype=jnp.int32) > block
    inputs = jnp.arange(block, dtype=jnp.int32)
    turns = freq_bins[:, None] * inputs[None, :] % period
    radians = turns.astype(jnp.float32) * (2.0 * math.pi / period)
    forward = jnp.where(sine_rows[:, None], jnp.sin(radians), jnp.cos(radians))
    moments = jnp.arange(period, dtype=jnp.int32)
    turns_back = moments[:, None] * freq_bins[None, :] % period
    radians_back = turns_back.astype(jnp.float32) * (2.0 * math.pi / period)
    border_bins = (freq_bins == 0) | (freq_bins == block)
    weights = jnp.where(border_bins, 1.0, 2.0) / period
    inverse = (
        jnp.where(sine_rows[None, :], jnp.sin(radians_back), jnp.cos(radians_back))
        * weights[None, :]
    )
    parity = jnp.where(freq_bins % 2 == 0, 1.0, -1.0).astype(jnp.float32)[:, None]
    return (forward, inverse, parity)


def to_spectra(blocks, table):
    return jnp.einsum(
        "fb,...bd->...fd", table, blocks.astype(jnp.float32), precision=lax.Precision.HIGHEST
    )


def from_spectra(table, spectra):
    return jnp.einsum("tf,...fd->...td", table, spectra, precision=lax.Precision.HIGHEST)


def spectral_product(left, right, block, conj_left):
    left_real = left[..., : block + 1, :]
    left_imag = left[..., block + 1 :, :]
    right_real = right[..., : block + 1, :]
    right_imag = right[..., block + 1 :, :]
    if conj_left:
        left_imag = -left_imag
    cross = left_imag * right_imag
    border = jnp.zeros_like(cross[..., :1, :])
    real_part = left_real * right_real - jnp.concatenate([border, cross, border], axis=-2)
    imag_part = left_real[..., 1:block, :] * right_imag + left_imag * right_real[..., 1:block, :]
    return jnp.concatenate([real_part, imag_part], axis=-2)


def on_device(value, gate_one, gate_two, filters, out_weight, grad_out):
    rows = value.shape[1]
    width = value.shape[2]
    seq_count = lax.axis_size("ctx")
    data_count = lax.axis_size("dp")
    position = lax.axis_index("ctx")
    block = math.gcd(rows, 128)
    own_blocks = rows // block
    lag_blocks = own_blocks * seq_count
    forward, inverse, parity = make_tables(block)
    low_rows = inverse[:block]
    high_rows = inverse[block:]
    first_block = position * own_blocks
    own_start = position * rows
    filter_blocks = filters.reshape(2, lag_blocks, block, width)
    filter_spectra = to_spectra(filter_blocks, forward)
    padded_filters = jnp.concatenate([jnp.zeros_like(filter_spectra), filter_spectra], axis=1)

    def piece_spectra_of(piece):
        count = piece.shape[0] // block
        return to_spectra(piece.reshape(count, block, width), forward)

    def causal(source, padded_filter):
        initial = jnp.zeros((own_blocks + 1, 2 * block, width), jnp.float32)
        piece = lax.all_gather(source, "ctx", axis=0, tiled=True)
        start = jnp.int32(0)

        def work(total):
            piece_spectra = piece_spectra_of(piece)
            count = piece_spectra.shape[0]
            start_block = start // block
            last_block = start_block + count - 1
            terms_list = []
            for index in range(own_blocks + 1):
                out_block = first_block - 1 + index
                anchor = jnp.maximum(out_block, 0)
                window = lax.dynamic_slice_in_dim(
                    padded_filter, lag_blocks + anchor - last_block, count, 0
                )
                window = jnp.flip(window, 0)
                summed_term = jnp.sum(spectral_product(window, piece_spectra, block, False), axis=0)
                if index == 0:
                    summed_term = summed_term * (out_block >= 0).astype(jnp.float32)
                terms_list.append(summed_term)
            return total + jnp.stack(terms_list)

        summed = lax.cond(start < own_start + rows, work, lambda total: total, initial)
        lower = from_spectra(low_rows, summed[1:])
        upper = from_spectra(high_rows, summed[:-1])
        return (lower + upper).reshape(rows, width)

    def anti_owner(source, grad_rows, padded_filter):
        filter_spectrum = padded_filter[lag_blocks:]
        whole_source, whole_grad = (
            lax.all_gather(source, "ctx", axis=0, tiled=True),
            lax.all_gather(grad_rows, "ctx", axis=0, tiled=True),
        )
        source_spectra = piece_spectra_of(whole_source)
        grad_spectra = piece_spectra_of(whole_grad)
        following = (
            jnp.concatenate([grad_spectra[1:], jnp.zeros_like(grad_spectra[:1])], axis=0) * parity
        )
        combined = grad_spectra + following
        padded = jnp.concatenate([combined, jnp.zeros_like(combined)], axis=0)

        def one_block(offset):
            window = lax.dynamic_slice_in_dim(padded, offset, lag_blocks, 0)
            grad_piece = jnp.sum(spectral_product(filter_spectrum, window, block, True), axis=0)
            lag_piece = jnp.sum(spectral_product(source_spectra, window, block, True), axis=0)
            return (grad_piece, lag_piece)

        grad_parts, lag_parts = lax.map(
            one_block, first_block + jnp.arange(own_blocks, dtype=jnp.int32)
        )
        grad_part = from_spectra(low_rows, grad_parts).reshape(rows, width)
        lag_part = from_spectra(low_rows, lag_parts).reshape(rows, width)
        return (grad_part, lag_part)

    def backward(source, grad_rows, padded_filter):
        return anti_owner(source, grad_rows, padded_filter)

    value_rows = value[0]
    gate_first = gate_one[0].astype(jnp.float32)
    gate_second = gate_two[0].astype(jnp.float32)
    cotangent = grad_out[0]
    first_conv = causal(value_rows, padded_filters[0])
    mixed_input = (gate_first * first_conv).astype(jnp.bfloat16)
    second_conv = causal(mixed_input, padded_filters[1])
    gated = (gate_second * second_conv).astype(jnp.bfloat16)
    mixed = jnp.dot(gated, out_weight, preferred_element_type=jnp.float32).astype(jnp.bfloat16)
    grad_gated = lax.dot_general(
        cotangent, out_weight, (((1,), (1,)), ((), ())), preferred_element_type=jnp.float32
    )
    grad_gate_two = (grad_gated * second_conv).astype(jnp.bfloat16)
    grad_second = (grad_gated * gate_second).astype(jnp.bfloat16)
    grad_mixed, lag_second = backward(mixed_input, grad_second, padded_filters[1])
    grad_gate_one = (grad_mixed * first_conv).astype(jnp.bfloat16)
    grad_first = (grad_mixed * gate_first).astype(jnp.bfloat16)
    grad_value_full, lag_first = backward(value_rows, grad_first, padded_filters[0])
    grad_value = grad_value_full.astype(jnp.bfloat16)
    own_lags = jnp.stack([lag_first, lag_second])
    filter_grad = (
        lax.psum_scatter(
            own_lags.astype(jnp.bfloat16), "dp", scatter_dimension=2, tiled=True
        ).astype(jnp.float32)
        / data_count
    )
    weight_part = lax.psum_scatter(
        lax.dot_general(
            gated, cotangent, (((0,), (0,)), ((), ())), preferred_element_type=jnp.float32
        ).astype(jnp.bfloat16),
        "dp",
        scatter_dimension=0,
        tiled=True,
    )
    weight_grad = (
        lax.psum_scatter(weight_part, "ctx", scatter_dimension=1, tiled=True).astype(jnp.float32)
        / data_count
    )
    return (
        mixed[None],
        grad_value[None],
        grad_gate_one[None],
        grad_gate_two[None],
        filter_grad,
        weight_grad,
    )


def solution(mesh):
    return jax.shard_map(
        on_device,
        mesh=mesh,
        in_specs=(
            P("dp", "ctx", None),
            P("dp", "ctx", None),
            P("dp", "ctx", None),
            P(),
            P(),
            P("dp", "ctx", None),
        ),
        out_specs=(
            P("dp", "ctx", None),
            P("dp", "ctx", None),
            P("dp", "ctx", None),
            P("dp", "ctx", None),
            P(None, "ctx", "dp"),
            P("dp", "ctx"),
        ),
        check_vma=False,
    )
```

profile of v0, /device:TPU:1, one launch (start us, length us, event | category | flops | bytes accessed | tf_op | source)
XLA Modules:
  0.0 463.9 jit_solution(18322438985190754017)
XLA Ops:
  9.2 4.0 convolution_bitcast_fusion.2
  13.1 8.0 %concatenate.92 = f32[2,16,256,512]{3,2,1,0:T(8,128)} pad(f32[2,8,256,512]{3,2,1,0:T(8,128)S(1)} %convolution_bitcast_fusion.2, f32[]{:T(128)} %constant.162.clone.1), padding=0_0x8_0x0_0x0_0 | pad | bytes 25165828 | tf_op jit(solution)/shard_map/concatenate | solution.py:72
  23.7 23.3 %all-gather.10.cloned.1.call-done = bf16[1,1024,512]{2,1,0:T(8,128)(2,1)} async-done(((bf16[1,128,512]{2,1,0:T(8,128)(2,1)}), bf16[1,1024,512]{2,1,0:T(8,128)(2,1)}) %all-gather.10.cloned.1.call-update) | async-done | bytes 1048592 | tf_op jit(solution)/shard_map/all_gather | solution.py:80
  47.0 27.0 %conditional.2 = (f32[2,256,512]{2,1,0:T(8,128)S(1)}) conditional(s32[]{:T(128)} %convert_element_type.91, () %tuple.25, (f32[2,16,256,512]{3,2,1,0:T(8,128)}, s32[]{:T(128)}, bf16[1024,512]{1,0:T(8,128)(2,1)}, f32[256,128]{1,0:T(8,128)}) %tuple.88), branch_computations={%region_0.1_spmd, %region_1.4_spmd} | conditional | flops 1623326720 | bytes 141476128 | solution.py:102
  47.0 4.4 slice.174
  54.6 3.8 fusion.87
  58.4 3.1 convolution_bitcast_fusion
  61.6 7.3 %reverse_multiply_fusion.1 = (f32[8,127,512]{2,1,0:T(8,128)}, f32[8,127,512]{2,1,0:T(8,128)S(1)}, f32[8,127,512]{2,1,0:T(8,128)}, f32[8,127,512]{2,1,0:T(8,128)}) fusion(f32[8,127,512]{2,1,0:T(8,128)S(1)} %copy-done.12, f32[8,256,512]{2,1,0:T(8,128)S(1)} %convolution_bitcast_fusion, f32[8,127,512]{2,1,0:T(8,128)} %get-tuple-element.115, ...), kind=kLoop, calls=%fused_computation.14 | loop fusion | flops 4161536 | bytes 20807680 | tf_op jit(solution)/shard_map/cond/branch_1_fun/mul | solution.py:49
  68.9 3.8 fusion
  77.3 37.7 %all-gather.12.cloned.1.call-done = bf16[1,1024,512]{1,2,0:T(8,128)(2,1)} async-done(((bf16[1,128,512]{1,2,0:T(8,128)(2,1)}), bf16[1,1024,512]{1,2,0:T(8,128)(2,1)}) %all-gather.12.cloned.1.call-update) | async-done | bytes 1048592 | tf_op jit(solution)/shard_map/all_gather | solution.py:80
  115.0 32.5 %conditional.3 = (f32[2,256,512]{2,1,0:T(8,128)S(1)}) conditional(s32[]{:T(128)} %convert_element_type.91, () %tuple.24, (f32[2,16,256,512]{3,2,1,0:T(8,128)}, s32[]{:T(128)}, bf16[1024,512]{0,1:T(8,128)(2,1)}, f32[256,128]{1,0:T(8,128)}) %tuple.87), branch_computations={%region_4.5_spmd, %region_5.8_spmd} | conditional | flops 1623326720 | bytes 147833088 | solution.py:102
  116.5 3.0 convolution_bitcast_fusion.1
  119.5 4.4 slice.190
  123.9 3.1 dynamic-slice_bitcast_fusion.3
  130.7 3.8 fusion.89
  134.5 7.9 %reverse_multiply_fusion.3 = (f32[8,127,512]{2,1,0:T(8,128)}, f32[8,127,512]{2,1,0:T(8,128)S(1)}, f32[8,127,512]{2,1,0:T(8,128)}, f32[8,127,512]{2,1,0:T(8,128)}) fusion(f32[8,127,512]{2,1,0:T(8,128)} %get-tuple-element.130, f32[8,256,512]{2,1,0:T(8,128)S(1)} %convolution_bitcast_fusion.1, f32[8,127,512]{2,1,0:T(8,128)} %get-tuple-element.131, ...), kind=kLoop, calls=%fused_computation.32 | loop fusion | flops 4161536 | bytes 20807680 | tf_op jit(solution)/shard_map/cond/branch_1_fun/mul | solution.py:49
  142.5 3.8 fusion.3
  153.0 8.2 %slice_bitcast_fusion = (f32[8,256,512]{2,1,0:T(8,128)}, f32[8,256,512]{2,1,0:T(8,128)}) fusion(f32[2,8,256,512]{3,2,1,0:T(8,128)} %copy-done.2), kind=kLoop, calls=%fused_computation.50 | loop fusion | bytes 16777216 | tf_op jit(solution)/shard_map/slice | solution.py:108
  161.7 4.5 convolution_bitcast_fusion.3
  166.3 72.9 %reduce-scatter.8.cloned.1.call-done = bf16[16,512]{1,0:T(8,128)(2,1)} async-done(((bf16[512,512]{1,0:T(8,128)(2,1)}), bf16[16,512]{1,0:T(8,128)(2,1)}) %reduce-scatter.8.cloned.1.call-update) | async-done | bytes 16400 | tf_op jit(solution)/shard_map/reduce_scatter | solution.py:163
  240.8 36.2 %all-gather.8.cloned.1.call-done = bf16[1024,512]{0,1:T(8,128)(2,1)} async-done(((bf16[128,512]{0,1:T(8,128)(2,1)}), bf16[1024,512]{0,1:T(8,128)(2,1)}) %all-gather.8.cloned.1.call-update) | async-done | bytes 1048592 | tf_op jit(solution)/shard_map/all_gather | solution.py:111
  278.4 2.6 convolution_bitcast_fusion.6
  285.1 3.8 fusion.17
  288.9 3.6 fusion.9
  292.6 3.8 maximum_reduce_fusion.4
  298.4 5.1 %convolution_bitcast_fusion.4 = f32[8,256,512]{2,1,0:T(8,128)} fusion(bf16[8,128,512]{2,1,0:T(8,128)(2,1)S(1)} %bitcast.158, s32[256]{0:T(256)} %copy-done.28, pred[256]{0:T(512)(128)(4,1)} %copy-done.30), kind=kOutput, calls=%fused_computation.68 | convolution fusion | flops 1611104256 | bytes 5244160 | tf_op jit(solution)/shard_map/fb,...bd->...fd/dot_general | solution.py:33
  305.2 9.6 %reduce-scatter.10.cloned.1.call-done = bf16[64,16]{1,0:T(8,128)(2,1)} async-done(((bf16[512,16]{1,0:T(8,128)(2,1)}), bf16[64,16]{1,0:T(8,128)(2,1)}) %reduce-scatter.10.cloned.1.call-update) | async-done | bytes 2064
  316.6 38.7 %all-gather.14.cloned.1.call-done = bf16[1,1024,512]{1,2,0:T(8,128)(2,1)} async-done(((bf16[1,128,512]{1,2,0:T(8,128)(2,1)}), bf16[1,1024,512]{1,2,0:T(8,128)(2,1)}) %all-gather.14.cloned.1.call-update) | async-done | bytes 1048592 | tf_op jit(solution)/shard_map/all_gather | solution.py:111
  363.7 3.1 fusion.16
  366.8 4.4 fusion.8
  374.9 3.0 maximum_reduce_fusion.5
  379.7 75.8 %reduce-scatter.6.cloned.1.call-done = bf16[2,128,16]{1,2,0:T(8,128)(2,1)} async-done(((bf16[2,128,512]{1,2,0:T(8,128)(2,1)}), bf16[2,128,16]{1,2,0:T(8,128)(2,1)}) %reduce-scatter.6.cloned.1.call-update) | async-done | bytes 8208 | tf_op jit(solution)/shard_map/reduce_scatter | solution.py:158
  (136 shorter events, 52.3 us)
Async XLA Ops:
  7.2 39.8 %all-gather.10.cloned.1.call-start = ((), (), s32[]{:S(2)}) async-start(), calls=%async_computation.6 | async-start | bytes 1179648 | tf_op jit(solution)/shard_map/all_gather | solution.py:80
  7.9 107.1 %all-gather.12.cloned.1.call-start = ((), (), s32[]{:S(2)}) async-start(), calls=%async_computation.7 | async-start | bytes 1179648 | tf_op jit(solution)/shard_map/all_gather | solution.py:80
  9.0 66.4 %copy-start.21 = (bf16[1,128,512]{1,2,0:T(8,128)(2,1)}, bf16[1,128,512]{1,2,0:T(8,128)(2,1)S(1)}, u32[]{:S(2)}) copy-start(bf16[1,128,512]{1,2,0:T(8,128)(2,1)S(1)} %copy.24) | copy-start | bytes 393220
  9.0 269.4 %copy-start.30 = (pred[256]{0:T(512)(128)(4,1)}, pred[256]{0:T(512)(128)(4,1)S(1)}, u32[]{:S(2)}) copy-start(pred[256]{0:T(512)(128)(4,1)S(1)} %iota_compare_fusion) | copy-start | bytes 772
  9.1 269.3 %copy-start.28 = (s32[256]{0:T(256)}, s32[256]{0:T(256)S(1)}, u32[]{:S(2)}) copy-start(s32[256]{0:T(256)S(1)} %get-tuple-element.103) | copy-start | bytes 3076
  9.1 272.5 %copy-start.32 = (f32[256]{0:T(256)}, f32[256]{0:T(256)S(1)}, u32[]{:S(2)}) copy-start(f32[256]{0:T(256)S(1)} %get-tuple-element.102) | copy-start | bytes 3076
  13.1 8.3 %copy-start.2 = (f32[2,8,256,512]{3,2,1,0:T(8,128)}, f32[2,8,256,512]{3,2,1,0:T(8,128)S(1)}, u32[]{:S(2)}) copy-start(f32[2,8,256,512]{3,2,1,0:T(8,128)S(1)} %convolution_bitcast_fusion.2) | copy-start | bytes 25165828
  54.6 3.8 copy-start.17
  61.6 7.3 %copy-start.8 = (f32[8,129,512]{2,1,0:T(8,128)S(1)}, f32[8,129,512]{2,1,0:T(8,128)}, u32[]{:S(2)}) copy-start(f32[8,129,512]{2,1,0:T(8,128)} %slice.272) | copy-start | bytes 6340612 | tf_op jit(solution)/shard_map/cond
  68.9 3.8 copy-start.10
  77.2 162.1 %reduce-scatter.8.cloned.1.call-start = ((), (), s32[]{:S(2)}) async-start(), calls=%async_computation.5 | async-start | bytes 540672 | tf_op jit(solution)/shard_map/reduce_scatter | solution.py:163
  134.5 7.9 %copy-start.9 = (f32[8,129,512]{2,1,0:T(8,128)S(1)}, f32[8,129,512]{2,1,0:T(8,128)}, u32[]{:S(2)}) copy-start(f32[8,129,512]{2,1,0:T(8,128)} %slice.281) | copy-start | bytes 6340612 | tf_op jit(solution)/shard_map/cond
  142.4 3.8 copy-start.11
  147.5 4.4 copy-start.19
  147.5 4.3 copy-start.26
  151.8 125.1 %all-gather.8.cloned.1.call-start = ((), (), s32[]{:S(2)}) async-start(), calls=%async_computation.3 | async-start | bytes 1179648 | tf_op jit(solution)/shard_map/all_gather | solution.py:111
  152.9 162.0 %reduce-scatter.10.cloned.1.call-start = ((), (), s32[]{:S(2)}) async-start(), calls=%async_computation.9 | async-start | bytes 147456
  152.9 8.2 %copy-start.13 = (bf16[1,1024,512]{1,2,0:T(8,128)(2,1)S(1)}, bf16[1,1024,512]{1,2,0:T(8,128)(2,1)}, u32[]{:S(2)}) copy-start(bf16[1,1024,512]{1,2,0:T(8,128)(2,1)} %all-gather.12.cloned.1.call-done) | copy-start | bytes 3145732
  240.7 114.7 %all-gather.14.cloned.1.call-start = ((), (), s32[]{:S(2)}) async-start(), calls=%async_computation.8 | async-start | bytes 1179648 | tf_op jit(solution)/shard_map/all_gather | solution.py:111
  281.7 3.5 copy-start.6
  292.6 3.8 copy-start.22
  292.6 3.8 copy-start.23
  292.6 5.8 %copy-start.16 = (bf16[1,1024,512]{2,1,0:T(8,128)(2,1)S(1)}, bf16[1,1024,512]{2,1,0:T(8,128)(2,1)}, u32[]{:S(2)}) copy-start(bf16[1,1024,512]{2,1,0:T(8,128)(2,1)} %all-gather.10.cloned.1.call-done) | copy-start | bytes 3145732
  298.1 157.4 %reduce-scatter.6.cloned.1.call-start = ((), (), s32[]{:S(2)}) async-start(), calls=%async_computation.4 | async-start | bytes 270336 | tf_op jit(solution)/shard_map/reduce_scatter | solution.py:158
  298.4 5.2 %copy-start.24 = (bf16[1,128,512]{1,2,0:T(8,128)(2,1)S(1)}, bf16[1,128,512]{1,2,0:T(8,128)(2,1)}, u32[]{:S(2)}) copy-start(bf16[1,128,512]{1,2,0:T(8,128)(2,1)} %get-tuple-element.154) | copy-start | bytes 393220
  298.4 6.0 %copy-start.15 = (f32[512,128]{1,0:T(8,128)S(1)}, f32[512,128]{1,0:T(8,128)}, u32[]{:S(2)}) copy-start(f32[512,128]{1,0:T(8,128)} %copy-done.14) | copy-start | bytes 786436
  298.4 6.0 %copy-start.20 = (bf16[512,512]{1,0:T(8,128)(2,1)S(1)}, bf16[512,512]{1,0:T(8,128)(2,1)}, u32[]{:S(2)}) copy-start(bf16[512,512]{1,0:T(8,128)(2,1)} %param.14) | copy-start | bytes 1572868
  298.4 17.2 %copy-start.18 = (f32[256,512]{1,0:T(8,128)S(1)}, f32[256,512]{1,0:T(8,128)}, u32[]{:S(2)}) copy-start(f32[256,512]{1,0:T(8,128)} %get-tuple-element.161) | copy-start | bytes 1572868
  303.5 53.3 %copy-start.29 = (s32[256]{0:T(256)S(1)}, s32[256]{0:T(256)}, u32[]{:S(2)}) copy-start(s32[256]{0:T(256)} %copy-done.28) | copy-start | bytes 3076
  303.5 53.3 %copy-start.31 = (pred[256]{0:T(512)(128)(4,1)S(1)}, pred[256]{0:T(512)(128)(4,1)}, u32[]{:S(2)}) copy-start(pred[256]{0:T(512)(128)(4,1)} %copy-done.30) | copy-start | bytes 772
  360.2 3.5 copy-start.5
  374.9 81.9 %copy-start.1 = (bf16[2,1024,512]{2,1,0:T(8,128)(2,1)S(1)}, bf16[2,1024,512]{2,1,0:T(8,128)(2,1)}, u32[]{:S(2)}) copy-start(bf16[2,1024,512]{2,1,0:T(8,128)(2,1)} %param.13) | copy-start | bytes 6291460
  (9 other events, 21.8 us)
Sparse Core Ops, SparseCore 0:
  9.8 37.1 all-gather.9
  77.3 37.6 all-gather.11
  151.9 87.2 reduce-scatter.7
  241.4 35.5 all-gather.7
  279.3 35.5 reduce-scatter.9
  317.0 38.3 all-gather.13
  373.6 81.8 reduce-scatter.5
where the time goes:
time: 469 us; the launch traced here: 464 us
  waiting for transfers between devices  295 us (63%)
  local copies, waits for them, and re-layouts  59.8 us (13%)
  other arithmetic  54.6 us (12%)
  matrix products  39 us (8%)
  between operations  14.8 us (3%)
    reduce_scatter x1, waiting for transfers between devices, on_device(): lax.psum_scatter(own_lags.astype(jnp.bfloat16), 'dp', scatter_dimension=2...  75.8 us
    all_gather x2, waiting for transfers between devices, anti_owner(): lax.all_gather(grad_rows, 'ctx', axis=0, tiled=True)  74.9 us
    reduce_scatter x1, waiting for transfers between devices, on_device(): lax.psum_scatter(lax.dot_general(gated, cotangent, (((0,), (0,)), ((), ()...  72.9 us
    all_gather x2, waiting for transfers between devices, causal(): piece = lax.all_gather(source, 'ctx', axis=0, tiled=True)  60.9 us
    dot_general x7, matrix products, to_spectra(): jnp.einsum('fb,...bd->...fd', table, blocks.astype(jnp.float32), precisio...  25 us
    mul x4, other arithmetic, spectral_product(): cross = left_imag * right_imag  22 us
    sub x4, other arithmetic, spectral_product(): left_real * right_real - jnp.concatenate([border, cross, border], axis=-2)  15.5 us
    unnamed x61, local copies, waits for them, and re-layouts  10.9 us
  transfers between devices with their start and end apart: 7, of which 7 were waited for; matrix products, arithmetic and copies ran while one was open for 14% of the time, Pallas kernels for 0%

commit v1 on v0

v1 whole, which is shorter than its diff:
```python
import numpy as np

import jax
import jax.numpy as jnp
from jax import lax
from jax.experimental import pallas as pl
from jax.experimental.pallas import tpu as pltpu
from jax.sharding import PartitionSpec as P

F32 = jnp.float32
BF16 = jnp.bfloat16
MESH = pl.DeviceIdType.MESH

CTX = 8
CHIPS = 16
WIDTH = 512
ROWS = 128
BLK = 256
BINS = 256
CHUNK = 16


def tables():
    bins = np.concatenate([np.arange(0, BINS, 2), np.arange(1, BINS, 2)])
    angle = 2.0 * np.pi * (bins[:, None] + 0.5) * np.arange(BLK)[None, :] / (2 * BLK)
    forward = np.concatenate([np.cos(angle), -np.sin(angle)], axis=0)
    inverse = forward.T / BINS

    def split(table):
        high = table.astype(BF16)
        low = (table - high.astype(np.float64)).astype(BF16)
        return high, low

    return split(forward) + split(inverse)


def lanes_low(rows):
    return lax.broadcasted_iota(jnp.int32, (rows, 128), 1) < 64


def turn(x, shift=64):
    return pltpu.roll(x, shift, 1)


def mix(a, b):
    low = lanes_low(a.shape[0])
    return jnp.where(low, a, turn(b)), jnp.where(low, turn(a), b)


def kernel(
    value, gate_one, gate_two, grad_out, filters, weight, fh, fl, ih, il,
    mixed, grad_value, grad_gate_one, grad_gate_two, filter_grad, weight_grad,
    sbuf, rbuf, filt, g_first, g_second, v_spec, m_spec, s_spec, f_spec, p_high, p_low,
    first_conv, grad_gated, xt,
    w_part, w_pair, w_sum, w_plane, w_tiles, w_ring,
    f_part, f_pair, f_sum, f_plane, f_send, f_recv,
    filt_sem, z_send, z_recv, pair_send, pair_recv, plane_send, plane_recv,
    ring_send, ring_recv, swap_send, swap_recv,
):
    doc = lax.axis_index("dp")
    pos = lax.axis_index("ctx")
    core = lax.rem(doc, 2)
    chip = lax.div(doc, 2)
    swap_doc = 4 * pos + lax.rem(doc, 4)
    swap_pos = lax.div(doc, 4)
    swap_self = swap_pos == pos

    column = pl.multiple_of(lax.div(pos, 2) * 128, 128)
    filt_copy = pltpu.make_async_copy(filters.at[:, :, pl.ds(column, 128)], filt, filt_sem)
    filt_copy.start()

    barrier = pltpu.get_barrier_semaphore()
    for o in range(1, CTX):
        pl.semaphore_signal(barrier, inc=1, device_id=(doc, lax.rem(pos + o, CTX)), device_id_type=MESH)
    pl.semaphore_signal(barrier, inc=1, device_id=(2 * chip + 1 - core, pos), device_id_type=MESH)
    for o in range(1, CHIPS):
        peer = 2 * lax.rem(chip + o, CHIPS) + core
        pl.semaphore_signal(barrier, inc=1, device_id=(peer, pos), device_id_type=MESH)

    @pl.when(jnp.logical_not(swap_self))
    def _():
        pl.semaphore_signal(barrier, inc=1, device_id=(swap_doc, swap_pos), device_id_type=MESH)

    def pack_rows(slot, tile_of):
        for p in range(4):
            first, second = mix(tile_of(0, p), tile_of(1, p))
            sbuf[slot, 2 * p] = first.astype(BF16)
            sbuf[slot, 2 * p + 1] = second.astype(BF16)
        rbuf[slot, pos] = sbuf[slot, pos]

    def pack_blocks(slot, tiles):
        for t in range(2):
            for h in range(2):
                part = tiles[t][128 * h : 128 * h + 128]
                first, second = mix(part[:64], part[64:])
                sbuf[slot, 4 * t + h] = first.astype(BF16)
                sbuf[slot, 4 * t + 2 + h] = second.astype(BF16)
        rbuf[slot, pos] = sbuf[slot, pos]

    def ring_copy(slot, to, at):
        return pltpu.make_async_remote_copy(
            src_ref=sbuf.at[slot, to],
            dst_ref=rbuf.at[slot, at],
            send_sem=z_send.at[slot, to],
            recv_sem=z_recv.at[slot, at],
            device_id=(doc, to),
            device_id_type=MESH,
        )

    def ring_start(slot):
        for o in (4, 3, 5, 2, 6, 1, 7):
            ring_copy(slot, lax.rem(pos + o, CTX), pos).start()

    def ring_wait(slot):
        for o in (1, 7, 2, 6, 3, 5, 4):
            src = lax.rem(pos + o, CTX)
            ring_copy(slot, src, src).wait_recv()

    def rows_tile(ref):
        return lambda h, p: ref[64 * h : 64 * h + 64, 128 * p : 128 * p + 128].astype(F32)

    pack_rows(0, rows_tile(value))
    pack_rows(1, rows_tile(gate_one))
    grad_gated[...] = lax.dot_general(
        grad_out[...], weight[...], (((1,), (1,)), ((), ())), preferred_element_type=F32
    )
    pack_rows(
        2,
        lambda h, p: (
            grad_gated[64 * h : 64 * h + 64, 128 * p : 128 * p + 128]
            * gate_two[64 * h : 64 * h + 64, 128 * p : 128 * p + 128].astype(F32)
        ).astype(BF16).astype(F32),
    )
    pl.semaphore_wait(barrier, 23 + jnp.where(swap_self, 0, 1))
    ring_start(0)
    ring_start(1)
    ring_start(2)

    def forward(spec):
        block = xt[...]
        spec[...] = jnp.dot(fh[...], block, preferred_element_type=F32) + jnp.dot(
            fl[...], block, preferred_element_type=F32
        )

    def inverse():
        high = p_high[...]
        return (
            jnp.dot(ih[...], high, preferred_element_type=F32)
            + jnp.dot(il[...], high, preferred_element_type=F32)
            + jnp.dot(ih[...], p_low[...], preferred_element_type=F32)
        )

    def load(spec, r):
        a = spec[pl.ds(r, CHUNK), :]
        b = spec[pl.ds(BINS + r, CHUNK), :]
        return (a[:, :128], b[:, :128]), (a[:, 128:], b[:, 128:])

    def store(r, low_blocks, high_blocks):
        for part in range(2):
            for t, block in enumerate((low_blocks, high_blocks)):
                x = block[part]
                high = x.astype(BF16)
                where = (pl.ds(part * BINS + r, CHUNK), slice(128 * t, 128 * t + 128))
                p_high[where] = high
                p_low[where] = (x - high.astype(F32)).astype(BF16)

    def both(x):
        return tuple(turn(part) for part in x)

    def pick(a, b):
        low = lanes_low(CHUNK)
        return tuple(jnp.where(low, x, y) for x, y in zip(a, b))

    def low_only(x):
        return pick(x, (jnp.zeros_like(x[0]),) * 2)

    def high_only(x):
        return pick((jnp.zeros_like(x[0]),) * 2, x)

    def times(a, b):
        return a[0] * b[0] - a[1] * b[1], a[0] * b[1] + a[1] * b[0]

    def conj_times(a, b):
        return a[0] * b[0] + a[1] * b[1], a[0] * b[1] - a[1] * b[0]

    def plus(*terms):
        return sum(t[0] for t in terms[1:]) + terms[0][0], sum(t[1] for t in terms[1:]) + terms[0][1]

    def chunks(body):
        for half, sign in ((0, 1.0), (1, -1.0)):

            def step(i, carry):
                body(pl.multiple_of(half * (BINS // 2) + i * CHUNK, CHUNK), sign)
                return carry

            lax.fori_loop(0, BINS // 2 // CHUNK, step, 0)

    def spread(g01, g23):
        t01, t23 = both(g01), both(g23)
        return pick(g01, t01), pick(t01, g01), pick(g23, t23), t01, t23

    def convolve(filter_spec, data_spec):
        def body(r, sign):
            g01, g23 = load(filter_spec, r)
            x01, x23 = load(data_spec, r)
            h0, h1, h2, _, _ = spread(g01, g23)
            x10, x32 = both(x01), both(x23)
            x12 = pick(x10, x32)
            out01 = plus(times(h0, x01), times(high_only(g01), x10))
            out23 = plus(times(h0, x23), times(h1, x12), times(h2, x01), times(high_only(g23), x10))
            store(r, out01, out23)

        chunks(body)

    def correlate(filter_spec, data_spec, windows):
        def body(r, sign):
            g01, g23 = load(filter_spec, r)
            y01, y23 = load(data_spec, r)
            if windows:
                t01, t23 = both(y01), both(y23)
                n01, n23 = pick(t01, t23), low_only(t23)
                y01 = (y01[0] + sign * n01[1], y01[1] - sign * n01[0])
                y23 = (y23[0] + sign * n23[1], y23[1] - sign * n23[0])
            h0, h1, h2, t01, t23 = spread(g01, g23)
            y10, y32 = both(y01), both(y23)
            y12 = pick(y10, y32)
            out01 = plus(
                conj_times(h0, y01), conj_times(h1, y12), conj_times(h2, y23), conj_times(low_only(t23), y32)
            )
            out23 = plus(conj_times(h0, y23), conj_times(low_only(t01), y32))
            store(r, out01, out23)

        chunks(body)

    filt_copy.wait()
    odd = lax.rem(pos, 2) == 1
    for which, spec in ((0, g_first), (1, g_second)):
        for t in range(2):
            lag_tiles = []
            for k in (2 * t, 2 * t + 1):
                tile = filt[which, BLK * k : BLK * k + BLK, :].astype(F32)
                lag_tiles.append(jnp.where(odd, turn(tile), tile))
            xt[:, 128 * t : 128 * t + 128] = mix(*lag_tiles)[0].astype(BF16)
        forward(spec)

        def window(r, sign, spec=spec):
            h01, h23 = load(spec, r)
            t01, t23 = both(h01), both(h23)
            b01, b23 = high_only(t01), pick(t01, t23)
            for t, (h, b) in enumerate(((h01, b01), (h23, b23))):
                spec[pl.ds(r, CHUNK), 128 * t : 128 * t + 128] = h[0] - sign * b[1]
                spec[pl.ds(BINS + r, CHUNK), 128 * t : 128 * t + 128] = h[1] + sign * b[0]

        chunks(window)

    def arrived(slot, t, h):
        return mix(rbuf[slot, 4 * t + h].astype(F32), rbuf[slot, 4 * t + 2 + h].astype(F32))

    def to_columns(slot, scale=None):
        for t in range(2):
            for h in range(2):
                for half, part in enumerate(arrived(slot, t, h)):
                    where = (
                        slice(128 * h + 64 * half, 128 * h + 64 * half + 64),
                        slice(128 * t, 128 * t + 128),
                    )
                    if scale is not None:
                        part = part * scale[where]
                    xt[where] = part.astype(BF16)

    def split_tiles(x):
        return x[:, :128], x[:, 128:]

    ring_wait(0)
    to_columns(0)
    forward(v_spec)
    convolve(g_first, v_spec)
    first_conv[...] = inverse()
    ring_wait(1)
    to_columns(1, first_conv)
    forward(m_spec)
    convolve(g_second, m_spec)
    pack_blocks(3, split_tiles(inverse()))
    ring_start(3)

    ring_wait(2)
    to_columns(2)
    forward(s_spec)
    correlate(g_second, s_spec, False)
    grad_mixed = inverse()
    pack_blocks(4, split_tiles(grad_mixed * first_conv[...]))
    ring_start(4)
    first_conv[...] = grad_mixed
    to_columns(1, first_conv)
    forward(f_spec)
    correlate(g_first, f_spec, False)
    pack_blocks(5, split_tiles(inverse()))
    ring_start(5)

    lane_group = lax.div(lax.broadcasted_iota(jnp.int32, (16, 128), 1), 16)
    for which, stream, grads in ((0, v_spec, f_spec), (1, m_spec, s_spec)):
        correlate(stream, grads, True)
        lags = inverse()
        for h in range(2):
            for t in range(2):
                part = lags[128 * h : 128 * h + 128, 128 * t : 128 * t + 128]
                groups = [part[16 * g : 16 * g + 16] for g in range(8)]
                for s in (4, 2, 1):
                    keep = lax.rem(lax.div(lane_group, s), 2) == 0
                    for g in range(8):
                        if g & s == 0:
                            a, b = groups[g], groups[g | s]
                            groups[g] = jnp.where(keep, a, turn(b, 16 * s))
                            groups[g | s] = jnp.where(keep, turn(a, 128 - 16 * s), b)
                for u in range(8):
                    lag_block = 2 * (2 * t + u // 4) + h
                    q = u % 4
                    f_part[q % 2, 2 * lag_block + q // 2, 16 * which : 16 * which + 16, :] = groups[u].astype(BF16)

    def pair_copy(index, src, dst):
        return pltpu.make_async_remote_copy(
            src_ref=src.at[1 - core],
            dst_ref=dst,
            send_sem=pair_send.at[index],
            recv_sem=pair_recv.at[index],
            device_id=(2 * chip + 1 - core, pos),
            device_id_type=MESH,
        )

    def plane_copy(index, src, dst, to, at):
        return pltpu.make_async_remote_copy(
            src_ref=src.at[to],
            dst_ref=dst.at[at],
            send_sem=plane_send.at[index, to],
            recv_sem=plane_recv.at[index, at],
            device_id=(2 * to + core, pos),
            device_id_type=MESH,
        )

    def plane_start(index, src, dst):
        for o in range(1, CHIPS):
            plane_copy(index, src, dst, lax.rem(chip + o, CHIPS), chip).start()

    def plane_wait(index, src, dst):
        for o in range(1, CHIPS):
            at = lax.rem(chip + o, CHIPS)
            plane_copy(index, src, dst, at, at).wait_recv()

    f_pair_copy = pair_copy(0, f_part, f_pair)
    f_pair_copy.start()

    def row_tile(slot, p):
        return mix(rbuf[slot, 2 * p].astype(F32), rbuf[slot, 2 * p + 1].astype(F32))

    ring_wait(3)
    for p in range(4):
        for half, part in enumerate(row_tile(3, p)):
            where = (slice(64 * half, 64 * half + 64), slice(128 * p, 128 * p + 128))
            grad_gate_two[where] = (grad_gated[where] * part).astype(BF16)
            grad_gated[where] = (gate_two[where].astype(F32) * part).astype(BF16).astype(F32)
    gated = grad_gated[...].astype(BF16)
    gated_t = grad_gated[...].T.astype(BF16)
    for c in range(4):
        part = jnp.dot(
            gated_t[128 * c : 128 * c + 128], grad_out[...], preferred_element_type=F32
        ).astype(BF16)
        for i in range(8):
            row = 16 * (4 * c + i // 2)
            w_part[i % 2, 4 * c + i // 2] = part[16 * i : 16 * i + 16]
    w_pair_copy = pair_copy(1, w_part, w_pair)
    w_pair_copy.start()
    mixed[...] = jnp.dot(gated, weight[...], preferred_element_type=F32).astype(BF16)

    f_pair_copy.wait_recv()
    f_sum[...] = (f_part[core].astype(F32) + f_pair[...].astype(F32)).astype(BF16)
    plane_start(0, f_sum, f_plane)
    f_plane[chip] = f_sum[chip]
    w_pair_copy.wait_recv()
    w_sum[...] = (w_part[core].astype(F32) + w_pair[...].astype(F32)).astype(BF16)
    plane_start(1, w_sum, w_plane)
    w_plane[chip] = w_sum[chip]

    for slot, out in ((4, grad_gate_one), (5, grad_value)):
        ring_wait(slot)
        for p in range(4):
            for half, part in enumerate(row_tile(slot, p)):
                out[64 * half : 64 * half + 64, 128 * p : 128 * p + 128] = part.astype(BF16)

    scale = 1.0 / 32

    plane_wait(0, f_sum, f_plane)
    f_send[...] = jnp.sum(f_plane[...].astype(F32), axis=0) * scale
    swap = pltpu.make_async_remote_copy(
        src_ref=f_send,
        dst_ref=f_recv,
        send_sem=swap_send,
        recv_sem=swap_recv,
        device_id=(swap_doc, swap_pos),
        device_id_type=MESH,
    )

    @pl.when(jnp.logical_not(swap_self))
    def _():
        swap.start()

    @pl.when(swap_self)
    def _():
        f_recv[...] = f_send[...]

    def tile_copy(to, at):
        return pltpu.make_async_remote_copy(
            src_ref=w_tiles.at[lax.div(to, 2)],
            dst_ref=w_ring.at[at],
            send_sem=ring_send.at[to],
            recv_sem=ring_recv.at[at],
            device_id=(doc, to),
            device_id_type=MESH,
        )

    plane_wait(1, w_sum, w_plane)
    w_total = jnp.sum(w_plane[...].astype(F32), axis=0).astype(BF16)
    for p in range(4):
        w_tiles[p] = w_total[:, 128 * p : 128 * p + 128]
    for o in (4, 3, 5, 2, 6, 1, 7):
        tile_copy(lax.rem(pos + o, CTX), pos).start()
    w_ring[pos] = w_tiles[lax.div(pos, 2)]
    for o in range(1, CTX):
        src = lax.rem(pos + o, CTX)
        tile_copy(src, src).wait_recv()
    total = jnp.sum(w_ring[...].astype(F32), axis=0) * scale
    weight_grad[...] = jnp.where(odd, turn(total), total)[:, :64]

    @pl.when(jnp.logical_not(swap_self))
    def _():
        swap.wait_recv()

    for which in range(2):
        packed = f_recv[16 * which : 16 * which + 16, :]
        for g in range(8):
            rows = packed if g == 0 else turn(packed, 128 - 16 * g)
            filter_grad[which, 16 * g : 16 * g + 16, :] = rows[:, :16]

    for slot in range(6):
        for o in range(1, CTX):
            ring_copy(slot, lax.rem(pos + o, CTX), pos).wait_send()
    f_pair_copy.wait_send()
    w_pair_copy.wait_send()
    for index, src, dst in ((0, f_sum, f_plane), (1, w_sum, w_plane)):
        for o in range(1, CHIPS):
            plane_copy(index, src, dst, lax.rem(chip + o, CHIPS), chip).wait_send()
    for o in range(1, CTX):
        tile_copy(lax.rem(pos + o, CTX), pos).wait_send()

    @pl.when(jnp.logical_not(swap_self))
    def _():
        swap.wait_send()


def on_device(value, gate_one, gate_two, filters, out_weight, grad_out):
    vmem = pl.BlockSpec(memory_space=pltpu.VMEM)
    stream = jax.ShapeDtypeStruct((ROWS, WIDTH), BF16)
    spectrum = pltpu.VMEM((2 * BINS, 256), F32)
    dma = pltpu.SemaphoreType.DMA
    outs = pl.pallas_call(
        kernel,
        out_shape=(
            stream,
            stream,
            stream,
            stream,
            jax.ShapeDtypeStruct((2, ROWS, 16), F32),
            jax.ShapeDtypeStruct((16, 64), F32),
        ),
        in_specs=[vmem] * 4 + [pl.BlockSpec(memory_space=pl.ANY)] + [vmem] * 5,
        out_specs=[vmem] * 6,
        scratch_shapes=[
            pltpu.VMEM((6, CTX, 64, 128), BF16),
            pltpu.VMEM((6, CTX, 64, 128), BF16),
            pltpu.VMEM((2, 1024, 128), BF16),
            spectrum, spectrum, spectrum, spectrum, spectrum, spectrum,
            pltpu.VMEM((2 * BINS, 256), BF16),
            pltpu.VMEM((2 * BINS, 256), BF16),
            pltpu.VMEM((BLK, 256), F32),
            pltpu.VMEM((ROWS, WIDTH), F32),
            pltpu.VMEM((BLK, 256), BF16),
            pltpu.VMEM((2, CHIPS, 16, WIDTH), BF16),
            pltpu.VMEM((CHIPS, 16, WIDTH), BF16),
            pltpu.VMEM((CHIPS, 16, WIDTH), BF16),
            pltpu.VMEM((CHIPS, 16, WIDTH), BF16),
            pltpu.VMEM((4, 16, 128), BF16),
            pltpu.VMEM((CTX, 16, 128), BF16),
            pltpu.VMEM((2, CHIPS, 32, 128), BF16),
            pltpu.VMEM((CHIPS, 32, 128), BF16),
            pltpu.VMEM((CHIPS, 32, 128), BF16),
            pltpu.VMEM((CHIPS, 32, 128), BF16),
            pltpu.VMEM((32, 128), F32),
            pltpu.VMEM((32, 128), F32),
            dma,
            dma((6, CTX)),
            dma((6, CTX)),
            dma((2,)),
            dma((2,)),
            dma((2, CHIPS)),
            dma((2, CHIPS)),
            dma((CTX,)),
            dma((CTX,)),
            dma,
            dma,
        ],
        compiler_params=pltpu.CompilerParams(collective_id=0, has_side_effects=True),
    )(
        value[0], gate_one[0], gate_two[0], grad_out[0], filters, out_weight,
        *(jnp.asarray(table) for table in tables()),
    )
    mixed, grad_value, grad_gate_one, grad_gate_two, filter_grad, weight_grad = outs
    return mixed[None], grad_value[None], grad_gate_one[None], grad_gate_two[None], filter_grad, weight_grad


def solution(mesh):
    stream = P("dp", "ctx", None)
    return jax.shard_map(
        on_device,
        mesh=mesh,
        in_specs=(stream, stream, stream, P(), P(), stream),
        out_specs=(stream, stream, stream, stream, P(None, "ctx", "dp"), P("dp", "ctx")),
        check_vma=False,
    )
```

time: 469 us -> 61.2 us (0.13); the launches traced: 464 us -> 60.9 us
  waiting for transfers between devices: 295 us -> 0 us
  other arithmetic: 54.6 us -> 0 us
  Pallas kernels: 0 us -> 51.2 us
  local copies, waits for them, and re-layouts: 59.8 us -> 9.14 us
  matrix products: 39 us -> 0 us
  between operations: 14.8 us -> 0.64 us
    reduce_scatter x2 -> x0, waiting for transfers between devices: 149 us -> none  [the longest x1 75.8 us: on_device(): lax.psum_scatter(own_lags.astype(jnp.bfloat16), 'dp', scatter_dimension=2...]
    all_gather x4 -> x0, waiting for transfers between devices: 136 us -> none  [the longest x2 74.9 us: anti_owner(): lax.all_gather(grad_rows, 'ctx', axis=0, tiled=True)]
    pallas_call x0 -> x1, Pallas kernels: none -> 51.2 us  [on_device(): pl.pallas_call(kernel, out_shape=(stream, stream, stream, stream, jax.Sha...]
    dot_general x18 -> x0, matrix products: 39 us -> none  [the longest x7 25 us: to_spectra(): jnp.einsum('fb,...bd->...fd', table, blocks.astype(jnp.float32), precisio...]
    slice x11 -> x0, local copies, waits for them, and re-layouts: 29.4 us -> none  [the longest x1 8.22 us: anti_owner(): filter_spectrum = padded_filter[lag_blocks:]]
    mul x7 -> x0, other arithmetic: 23.2 us -> none  [the longest x4 22 us: spectral_product(): cross = left_imag * right_imag]
    sub x4 -> x0, other arithmetic: 15.5 us -> none  [spectral_product(): left_real * right_real - jnp.concatenate([border, cross, border], axis=-2)]
    unnamed x8 -> x0, waiting for transfers between devices: 10.4 us -> none
  transfers between devices with their start and end apart: 7 -> 0, of which waited for: 7 -> 0; matrix products, arithmetic and copies ran while one was open for 14% -> 0% of each run, Pallas kernels for 0% -> 0%
where the time goes in v1:
time: 61.2 us; the launch traced here: 60.9 us
  Pallas kernels  51.2 us (84%)
  local copies, waits for them, and re-layouts  9.14 us (15%)
  between operations  0.64 us (1%)
    pallas_call x1, Pallas kernels, on_device(): pl.pallas_call(kernel, out_shape=(stream, stream, stream, stream, jax.Sha...  51.2 us
    unnamed x6, local copies, waits for them, and re-layouts  9.14 us

profile of v1, /device:TPU:1, one launch (start us, length us, event | category | flops | bytes accessed | tf_op | source)
XLA Modules:
  0.0 60.9 jit_solution(10677964407592779437)
XLA Ops:
  0.6 51.2 %shard_map.145 = (bf16[128,512]{1,0:T(8,128)(2,1)}, bf16[128,512]{1,0:T(8,128)(2,1)}, bf16[128,512]{1,0:T(8,128)(2,1)}, bf16[128,512]{1,0:T(8,128)(2,1)}, f32[2,128,16]{2,1,0:T(8,128)}, /*index=5*/f32[16,64]{1,0:T(8,128)}) custom-call(bf16[128,512]{1,0:T(8,128)(2,1)} %bitcast.8, bf16[128,512]{1,0:T(8,128)(2,1)} %bitcast.9, bf16[128,512]{1,0:T(8,128)(2,1)} %bitcast.10, ...), custom_call_target="tpu_custom_call" | custom-call | tf_op jit(solution)/shard_map/pallas_call | solution.py:464
  51.8 1.6 %copy.16 = f32[2,128,16]{1,2,0:T(8,128)} copy(f32[2,128,16]{2,1,0:T(8,128)} %get-tuple-element.22) | data formatting | bytes 32768
  53.4 1.6 %copy.22 = bf16[1,128,512]{2,1,0:T(8,128)(2,1)} copy(bf16[1,128,512]{2,1,0:T(8,128)(2,1)} %bitcast.15) | data formatting | bytes 262144
  54.9 1.6 %copy.23 = bf16[1,128,512]{2,1,0:T(8,128)(2,1)} copy(bf16[1,128,512]{2,1,0:T(8,128)(2,1)} %bitcast.14) | data formatting | bytes 262144
  56.5 1.6 %copy.24 = bf16[1,128,512]{2,1,0:T(8,128)(2,1)} copy(bf16[1,128,512]{2,1,0:T(8,128)(2,1)} %bitcast.13) | data formatting | bytes 262144
  58.1 1.6 %copy.25 = bf16[1,128,512]{2,1,0:T(8,128)(2,1)} copy(bf16[1,128,512]{2,1,0:T(8,128)(2,1)} %bitcast.12) | data formatting | bytes 262144
  59.6 1.3 %copy.26 = f32[16,64]{1,0:T(8,128)} copy(f32[16,64]{1,0:T(8,128)} %get-tuple-element.35) | data formatting | bytes 8192

commit v2 on v1

--- a/solution.py
+++ b/solution.py
@@ -18,6 +18,7 @@
 BLK = 256
 BINS = 256
 CHUNK = 16
+UNROLL = 8
 
 
 def tables():
@@ -31,7 +32,7 @@
         low = (table - high.astype(np.float64)).astype(BF16)
         return high, low
 
-    return split(forward) + split(inverse)
+    return split(forward) + split(inverse)[:1]
 
 
 def lanes_low(rows):
@@ -48,26 +49,20 @@
 
 
 def kernel(
-    value, gate_one, gate_two, grad_out, filters, weight, fh, fl, ih, il,
+    value_hbm, gate_one_hbm, gate_two_hbm, grad_out_hbm, filters_hbm, weight_hbm, fh_hbm, fl_hbm, ih_hbm,
     mixed, grad_value, grad_gate_one, grad_gate_two, filter_grad, weight_grad,
-    sbuf, rbuf, filt, g_first, g_second, v_spec, m_spec, s_spec, f_spec, p_high, p_low,
+    value, gate_one, gate_two, grad_out, weight, fh, fl, ih, filt,
+    sbuf, rbuf, g_first, g_second, v_spec, m_spec, s_spec, f_spec, product,
     first_conv, grad_gated, xt,
     w_part, w_pair, w_sum, w_plane, w_tiles, w_ring,
-    f_part, f_pair, f_sum, f_plane, f_send, f_recv,
-    filt_sem, z_send, z_recv, pair_send, pair_recv, plane_send, plane_recv,
-    ring_send, ring_recv, swap_send, swap_recv,
+    f_part, f_pair, f_sum, f_plane, f_send, f_recv, f_turned,
+    in_sem, z_send, z_recv, pair_send, pair_recv, plane_send, plane_recv,
+    ring_send, ring_recv, own_send, own_recv,
 ):
     doc = lax.axis_index("dp")
     pos = lax.axis_index("ctx")
     core = lax.rem(doc, 2)
     chip = lax.div(doc, 2)
-    swap_doc = 4 * pos + lax.rem(doc, 4)
-    swap_pos = lax.div(doc, 4)
-    swap_self = swap_pos == pos
-
-    column = pl.multiple_of(lax.div(pos, 2) * 128, 128)
-    filt_copy = pltpu.make_async_copy(filters.at[:, :, pl.ds(column, 128)], filt, filt_sem)
-    filt_copy.start()
 
     barrier = pltpu.get_barrier_semaphore()
     for o in range(1, CTX):
@@ -77,9 +72,21 @@
         peer = 2 * lax.rem(chip + o, CHIPS) + core
         pl.semaphore_signal(barrier, inc=1, device_id=(peer, pos), device_id_type=MESH)
 
-    @pl.when(jnp.logical_not(swap_self))
-    def _():
-        pl.semaphore_signal(barrier, inc=1, device_id=(swap_doc, swap_pos), device_id_type=MESH)
+    column = pl.multiple_of(lax.div(pos, 2) * 128, 128)
+    loads = {}
+    for i, (name, src, dst) in enumerate((
+        ("value", value_hbm, value),
+        ("filt", filters_hbm.at[:, :, pl.ds(column, 128)], filt),
+        ("fh", fh_hbm, fh),
+        ("fl", fl_hbm, fl),
+        ("gate_one", gate_one_hbm, gate_one),
+        ("grad_out", grad_out_hbm, grad_out),
+        ("weight", weight_hbm, weight),
+        ("gate_two", gate_two_hbm, gate_two),
+        ("ih", ih_hbm, ih),
+    )):
+        loads[name] = pltpu.make_async_copy(src, dst, in_sem.at[i])
+        loads[name].start()
 
     def pack_rows(slot, tile_of):
         for p in range(4):
@@ -119,22 +126,10 @@
     def rows_tile(ref):
         return lambda h, p: ref[64 * h : 64 * h + 64, 128 * p : 128 * p + 128].astype(F32)
 
+    loads["value"].wait()
     pack_rows(0, rows_tile(value))
-    pack_rows(1, rows_tile(gate_one))
-    grad_gated[...] = lax.dot_general(
-        grad_out[...], weight[...], (((1,), (1,)), ((), ())), preferred_element_type=F32
-    )
-    pack_rows(
-        2,
-        lambda h, p: (
-            grad_gated[64 * h : 64 * h + 64, 128 * p : 128 * p + 128]
-            * gate_two[64 * h : 64 * h + 64, 128 * p : 128 * p + 128].astype(F32)
-        ).astype(BF16).astype(F32),
-    )
-    pl.semaphore_wait(barrier, 23 + jnp.where(swap_self, 0, 1))
+    pl.semaphore_wait(barrier, CTX + CHIPS - 1)
     ring_start(0)
-    ring_start(1)
-    ring_start(2)
 
     def forward(spec):
         block = xt[...]
@@ -142,27 +137,18 @@
             fl[...], block, preferred_element_type=F32
         )
 
-    def inverse():
-        high = p_high[...]
-        return (
-            jnp.dot(ih[...], high, preferred_element_type=F32)
-            + jnp.dot(il[...], high, preferred_element_type=F32)
-            + jnp.dot(ih[...], p_low[...], preferred_element_type=F32)
-        )
+    def inverse(slot=0):
+        return jnp.dot(ih[...], product[slot], preferred_element_type=F32)
 
     def load(spec, r):
         a = spec[pl.ds(r, CHUNK), :]
         b = spec[pl.ds(BINS + r, CHUNK), :]
         return (a[:, :128], b[:, :128]), (a[:, 128:], b[:, 128:])
 
-    def store(r, low_blocks, high_blocks):
+    def store(slot, r, low_blocks, high_blocks):
         for part in range(2):
             for t, block in enumerate((low_blocks, high_blocks)):
-                x = block[part]
-                high = x.astype(BF16)
-                where = (pl.ds(part * BINS + r, CHUNK), slice(128 * t, 128 * t + 128))
-                p_high[where] = high
-                p_low[where] = (x - high.astype(F32)).astype(BF16)
+                product[slot, pl.ds(part * BINS + r, CHUNK), 128 * t : 128 * t + 128] = block[part].astype(BF16)
 
     def both(x):
         return tuple(turn(part) for part in x)
@@ -193,7 +179,7 @@
                 body(pl.multiple_of(half * (BINS // 2) + i * CHUNK, CHUNK), sign)
                 return carry
 
-            lax.fori_loop(0, BINS // 2 // CHUNK, step, 0)
+            lax.fori_loop(0, BINS // 2 // CHUNK, step, 0, unroll=UNROLL)
 
     def spread(g01, g23):
         t01, t23 = both(g01), both(g23)
@@ -208,11 +194,11 @@
             x12 = pick(x10, x32)
             out01 = plus(times(h0, x01), times(high_only(g01), x10))
             out23 = plus(times(h0, x23), times(h1, x12), times(h2, x01), times(high_only(g23), x10))
-            store(r, out01, out23)
+            store(0, r, out01, out23)
 
         chunks(body)
 
-    def correlate(filter_spec, data_spec, windows):
+    def correlate(filter_spec, data_spec, windows, slot=0):
         def body(r, sign):
             g01, g23 = load(filter_spec, r)
             y01, y23 = load(data_spec, r)
@@ -228,13 +214,13 @@
                 conj_times(h0, y01), conj_times(h1, y12), conj_times(h2, y23), conj_times(low_only(t23), y32)
             )
             out23 = plus(conj_times(h0, y23), conj_times(low_only(t01), y32))
-            store(r, out01, out23)
+            store(slot, r, out01, out23)
 
         chunks(body)
 
-    filt_copy.wait()
     odd = lax.rem(pos, 2) == 1
-    for which, spec in ((0, g_first), (1, g_second)):
+
+    def filter_windows(which, spec):
         for t in range(2):
             lag_tiles = []
             for k in (2 * t, 2 * t + 1):
@@ -243,7 +229,7 @@
             xt[:, 128 * t : 128 * t + 128] = mix(*lag_tiles)[0].astype(BF16)
         forward(spec)
 
-        def window(r, sign, spec=spec):
+        def window(r, sign):
             h01, h23 = load(spec, r)
             t01, t23 = both(h01), both(h23)
             b01, b23 = high_only(t01), pick(t01, t23)
@@ -252,6 +238,26 @@
                 spec[pl.ds(BINS + r, CHUNK), 128 * t : 128 * t + 128] = h[1] + sign * b[0]
 
         chunks(window)
+
+    for name in ("filt", "fh", "fl", "gate_one"):
+        loads[name].wait()
+    pack_rows(1, rows_tile(gate_one))
+    filter_windows(0, g_first)
+    ring_start(1)
+    for name in ("grad_out", "weight", "gate_two", "ih"):
+        loads[name].wait()
+    grad_gated[...] = lax.dot_general(
+        grad_out[...], weight[...], (((1,), (1,)), ((), ())), preferred_element_type=F32
+    )
+    pack_rows(
+        2,
+        lambda h, p: (
+            grad_gated[64 * h : 64 * h + 64, 128 * p : 128 * p + 128]
+            * gate_two[64 * h : 64 * h + 64, 128 * p : 128 * p + 128].astype(F32)
+        ).astype(BF16).astype(F32),
+    )
+    ring_start(2)
+    filter_windows(1, g_second)
 
     def arrived(slot, t, h):
         return mix(rbuf[slot, 4 * t + h].astype(F32), rbuf[slot, 4 * t + 2 + h].astype(F32))
@@ -290,32 +296,8 @@
     grad_mixed = inverse()
     pack_blocks(4, split_tiles(grad_mixed * first_conv[...]))
     ring_start(4)
-    first_conv[...] = grad_mixed
-    to_columns(1, first_conv)
+    to_columns(1, grad_mixed)
     forward(f_spec)
-    correlate(g_first, f_spec, False)
-    pack_blocks(5, split_tiles(inverse()))
-    ring_start(5)
-
-    lane_group = lax.div(lax.broadcasted_iota(jnp.int32, (16, 128), 1), 16)
-    for which, stream, grads in ((0, v_spec, f_spec), (1, m_spec, s_spec)):
-        correlate(stream, grads, True)
-        lags = inverse()
-        for h in range(2):
-            for t in range(2):
-                part = lags[128 * h : 128 * h + 128, 128 * t : 128 * t + 128]
-                groups = [part[16 * g : 16 * g + 16] for g in range(8)]
-                for s in (4, 2, 1):
-                    keep = lax.rem(lax.div(lane_group, s), 2) == 0
-                    for g in range(8):
-                        if g & s == 0:
-                            a, b = groups[g], groups[g | s]
-                            groups[g] = jnp.where(keep, a, turn(b, 16 * s))
-                            groups[g | s] = jnp.where(keep, turn(a, 128 - 16 * s), b)
-                for u in range(8):
-                    lag_block = 2 * (2 * t + u // 4) + h
-                    q = u % 4
-                    f_part[q % 2, 2 * lag_block + q // 2, 16 * which : 16 * which + 16, :] = groups[u].astype(BF16)
 
     def pair_copy(index, src, dst):
         return pltpu.make_async_remote_copy(
@@ -346,6 +328,17 @@
             at = lax.rem(chip + o, CHIPS)
             plane_copy(index, src, dst, at, at).wait_recv()
 
+    correlate(v_spec, f_spec, True, 0)
+    correlate(m_spec, s_spec, True, 1)
+    for which in range(2):
+        lags = inverse(which).astype(BF16)
+        for h in range(2):
+            for t in range(2):
+                for g in range(8):
+                    row = 128 * h + 16 * g
+                    f_part[g % 2, 4 * (2 * h + t) + g // 2, 16 * which : 16 * which + 16, :] = lags[
+                        row : row + 16, 128 * t : 128 * t + 128
+                    ]
     f_pair_copy = pair_copy(0, f_part, f_pair)
     f_pair_copy.start()
 
@@ -369,16 +362,18 @@
             w_part[i % 2, 4 * c + i // 2] = part[16 * i : 16 * i + 16]
     w_pair_copy = pair_copy(1, w_part, w_pair)
     w_pair_copy.start()
-    mixed[...] = jnp.dot(gated, weight[...], preferred_element_type=F32).astype(BF16)
-
     f_pair_copy.wait_recv()
     f_sum[...] = (f_part[core].astype(F32) + f_pair[...].astype(F32)).astype(BF16)
     plane_start(0, f_sum, f_plane)
     f_plane[chip] = f_sum[chip]
+    correlate(g_first, f_spec, False)
+    pack_blocks(5, split_tiles(inverse()))
+    ring_start(5)
     w_pair_copy.wait_recv()
     w_sum[...] = (w_part[core].astype(F32) + w_pair[...].astype(F32)).astype(BF16)
     plane_start(1, w_sum, w_plane)
     w_plane[chip] = w_sum[chip]
+    mixed[...] = jnp.dot(gated, weight[...], preferred_element_type=F32).astype(BF16)
 
     for slot, out in ((4, grad_gate_one), (5, grad_value)):
         ring_wait(slot)
@@ -390,22 +385,37 @@
 
     plane_wait(0, f_sum, f_plane)
     f_send[...] = jnp.sum(f_plane[...].astype(F32), axis=0) * scale
-    swap = pltpu.make_async_remote_copy(
-        src_ref=f_send,
-        dst_ref=f_recv,
-        send_sem=swap_send,
-        recv_sem=swap_recv,
-        device_id=(swap_doc, swap_pos),
-        device_id_type=MESH,
-    )
-
-    @pl.when(jnp.logical_not(swap_self))
-    def _():
-        swap.start()
-
-    @pl.when(swap_self)
-    def _():
-        f_recv[...] = f_send[...]
+    piece_h = lax.div(doc, 16)
+    piece_t = lax.rem(lax.div(doc, 8), 2)
+    piece_g = lax.rem(doc, 8)
+
+    def owner(i):
+        return 4 * pos + i % 4, 2 * (2 * piece_t + i // 4) + piece_h
+
+    def own_copy(i, at):
+        to_doc, to_pos = owner(i)
+        return pltpu.make_async_remote_copy(
+            src_ref=f_send,
+            dst_ref=f_recv.at[at],
+            send_sem=own_send.at[i],
+            recv_sem=own_recv.at[at],
+            device_id=(to_doc, to_pos),
+            device_id_type=MESH,
+        )
+
+    def is_self(i):
+        to_doc, to_pos = owner(i)
+        return jnp.logical_and(to_doc == doc, to_pos == pos)
+
+    for i in range(8):
+
+        @pl.when(jnp.logical_not(is_self(i)))
+        def _():
+            own_copy(i, piece_g).start()
+
+        @pl.when(is_self(i))
+        def _():
+            f_recv[piece_g] = f_send[...]
 
     def tile_copy(to, at):
         return pltpu.make_async_remote_copy(
@@ -430,15 +440,20 @@
     total = jnp.sum(w_ring[...].astype(F32), axis=0) * scale
     weight_grad[...] = jnp.where(odd, turn(total), total)[:, :64]
 
-    @pl.when(jnp.logical_not(swap_self))
-    def _():
-        swap.wait_recv()
-
+    from_pos = lax.div(doc, 4)
+    first_doc = 16 * lax.rem(pos, 2) + 8 * lax.div(pos, 4)
+    for g in range(8):
+
+        @pl.when(jnp.logical_not(jnp.logical_and(from_pos == pos, first_doc + g == doc)))
+        def _():
+            own_copy(0, g).wait_recv()
+
+    group = 4 * lax.rem(lax.div(pos, 2), 2) + lax.rem(doc, 4)
     for which in range(2):
-        packed = f_recv[16 * which : 16 * which + 16, :]
-        for g in range(8):
-            rows = packed if g == 0 else turn(packed, 128 - 16 * g)
-            filter_grad[which, 16 * g : 16 * g + 16, :] = rows[:, :16]
+        rows = f_recv[:, 16 * which : 16 * which + 16, :].reshape(ROWS, 128)
+        f_turned[which] = rows.T
+    for which in range(2):
+        filter_grad[which] = f_turned[which, pl.ds(pl.multiple_of(16 * group, 16), 16), :]
 
     for slot in range(6):
         for o in range(1, CTX):
@@ -451,35 +466,45 @@
     for o in range(1, CTX):
         tile_copy(lax.rem(pos + o, CTX), pos).wait_send()
 
-    @pl.when(jnp.logical_not(swap_self))
-    def _():
-        swap.wait_send()
+    for i in range(8):
+
+        @pl.when(jnp.logical_not(is_self(i)))
+        def _():
+            own_copy(i, piece_g).wait_send()
+
+
+def finish(*refs):
+    sems = refs[12]
+    copies = [pltpu.make_async_copy(refs[i], refs[6 + i], sems.at[i]) for i in range(6)]
+    for copy in copies:
+        copy.start()
+    for copy in copies:
+        copy.wait()
 
 
 def on_device(value, gate_one, gate_two, filters, out_weight, grad_out):
     vmem = pl.BlockSpec(memory_space=pltpu.VMEM)
-    stream = jax.ShapeDtypeStruct((ROWS, WIDTH), BF16)
+    anywhere = pl.BlockSpec(memory_space=pl.ANY)
+    stream = pltpu.VMEM((ROWS, WIDTH), BF16)
+    table = pltpu.VMEM((2 * BINS, 256), BF16)
     spectrum = pltpu.VMEM((2 * BINS, 256), F32)
     dma = pltpu.SemaphoreType.DMA
+    shapes = [((ROWS, WIDTH), BF16)] * 4 + [((2, 16, ROWS), F32), ((16, 64), F32)]
     outs = pl.pallas_call(
         kernel,
-        out_shape=(
-            stream,
-            stream,
-            stream,
-            stream,
-            jax.ShapeDtypeStruct((2, ROWS, 16), F32),
-            jax.ShapeDtypeStruct((16, 64), F32),
-        ),
-        in_specs=[vmem] * 4 + [pl.BlockSpec(memory_space=pl.ANY)] + [vmem] * 5,
+        out_shape=tuple(pltpu.VMEM(*shape) for shape in shapes),
+        in_specs=[anywhere] * 9,
         out_specs=[vmem] * 6,
         scratch_shapes=[
+            stream, stream, stream, stream,
+            pltpu.VMEM((WIDTH, WIDTH), BF16),
+            table, table,
+            pltpu.VMEM((BLK, 2 * BINS), BF16),
+            pltpu.VMEM((2, 1024, 128), BF16),
             pltpu.VMEM((6, CTX, 64, 128), BF16),
             pltpu.VMEM((6, CTX, 64, 128), BF16),
-            pltpu.VMEM((2, 1024, 128), BF16),
             spectrum, spectrum, spectrum, spectrum, spectrum, spectrum,
-            pltpu.VMEM((2 * BINS, 256), BF16),
-            pltpu.VMEM((2 * BINS, 256), BF16),
+            pltpu.VMEM((2, 2 * BINS, 256), BF16),
             pltpu.VMEM((BLK, 256), F32),
             pltpu.VMEM((ROWS, WIDTH), F32),
             pltpu.VMEM((BLK, 256), BF16),
@@ -494,8 +519,9 @@
             pltpu.VMEM((CHIPS, 32, 128), BF16),
             pltpu.VMEM((CHIPS, 32, 128), BF16),
             pltpu.VMEM((32, 128), F32),
-            pltpu.VMEM((32, 128), F32),
-            dma,
+            pltpu.VMEM((8, 32, 128), F32),
+            pltpu.VMEM((2, ROWS, 128), F32),
+            dma((9,)),
             dma((6, CTX)),
             dma((6, CTX)),
             dma((2,)),
@@ -504,16 +530,26 @@
             dma((2, CHIPS)),
             dma((CTX,)),
             dma((CTX,)),
-            dma,
-            dma,
+            dma((8,)),
+            dma((8,)),
         ],
         compiler_params=pltpu.CompilerParams(collective_id=0, has_side_effects=True),
     )(
         value[0], gate_one[0], gate_two[0], grad_out[0], filters, out_weight,
         *(jnp.asarray(table) for table in tables()),
     )
+    outs = pl.pallas_call(
+        finish,
+        out_shape=tuple(jax.ShapeDtypeStruct(*shape) for shape in shapes),
+        in_specs=[vmem] * 6,
+        out_specs=[anywhere] * 6,
+        scratch_shapes=[dma((6,))],
+    )(*outs)
     mixed, grad_value, grad_gate_one, grad_gate_two, filter_grad, weight_grad = outs
-    return mixed[None], grad_value[None], grad_gate_one[None], grad_gate_two[None], filter_grad, weight_grad
+    return (
+        mixed[None], grad_value[None], grad_gate_one[None], grad_gate_two[None],
+        jnp.swapaxes(filter_grad, 1, 2), weight_grad,
+    )
 
 
 def solution(mesh):

time: 61.2 us -> 52.2 us (0.85)
  local copies, waits for them, and re-layouts: 9.14 us -> 3.79 us
  Pallas kernels: 51.2 us -> 47.6 us
    unnamed x6 -> x12, local copies, waits for them, and re-layouts: 9.14 us -> 3.79 us
    pallas_call x1 -> x2, Pallas kernels: 51.2 us -> 47.6 us  [the longest x1 45.7 us: on_device(): pl.pallas_call(kernel, out_shape=tuple((pltpu.VMEM(*shape) for shape in s...]
where the time goes in v2:
time: 52.2 us; the launch traced here: 52.1 us
  Pallas kernels  47.6 us (91%)
  local copies, waits for them, and re-layouts  3.79 us (7%)
  between operations  0.66 us (1%)
    pallas_call x1, Pallas kernels, on_device(): pl.pallas_call(kernel, out_shape=tuple((pltpu.VMEM(*shape) for shape in s...  45.7 us
    unnamed x12, local copies, waits for them, and re-layouts  3.79 us
    pallas_call x1, Pallas kernels, on_device(): pl.pallas_call(finish, out_shape=tuple((jax.ShapeDtypeStruct(*shape) for...  1.94 us

profile of v2, /device:TPU:1, one launch (start us, length us, event | category | flops | bytes accessed | tf_op | source)
XLA Modules:
  0.0 52.1 jit_solution(5083942189713853977)
XLA Ops:
  0.6 45.7 %shard_map.136 = (bf16[128,512]{1,0:T(8,128)(2,1)S(1)}, bf16[128,512]{1,0:T(8,128)(2,1)S(1)}, bf16[128,512]{1,0:T(8,128)(2,1)S(1)}, bf16[128,512]{1,0:T(8,128)(2...) custom-call(bf16[128,512]{1,0:T(8,128)(2,1)} %bitcast.9, bf16[128,512]{1,0:T(8,128)(2,1)} %bitcast.10, ...), custom_call_target="tpu_custom_call" | custom-call | tf_op jit(solution)/shard_map/pallas_call | solution.py:493
  46.3 0.0 copy-start
  46.3 0.6 %copy-done = bf16[128,512]{1,0:T(8,128)(2,1)} copy-done((bf16[128,512]{1,0:T(8,128)(2,1)}, bf16[128,512]{1,0:T(8,128)(2,1)S(1)}, u32[]{:S(2)}) %copy-start) | copy-done | bytes 131096
  47.0 0.0 copy-start.1
  47.0 0.7 %copy-done.1 = bf16[128,512]{1,0:T(8,128)(2,1)} copy-done((bf16[128,512]{1,0:T(8,128)(2,1)}, bf16[128,512]{1,0:T(8,128)(2,1)S(1)}, u32[]{:S(2)}) %copy-start.1) | copy-done | bytes 131096
  47.6 0.0 copy-start.2
  47.6 0.6 %copy-done.2 = bf16[128,512]{1,0:T(8,128)(2,1)} copy-done((bf16[128,512]{1,0:T(8,128)(2,1)}, bf16[128,512]{1,0:T(8,128)(2,1)S(1)}, u32[]{:S(2)}) %copy-start.2) | copy-done | bytes 131096
  48.3 0.0 copy-start.3
  48.3 0.6 %copy-done.3 = bf16[128,512]{1,0:T(8,128)(2,1)} copy-done((bf16[128,512]{1,0:T(8,128)(2,1)}, bf16[128,512]{1,0:T(8,128)(2,1)S(1)}, u32[]{:S(2)}) %copy-start.3) | copy-done | bytes 131096
  48.9 0.0 copy-start.4
  48.9 0.6 %copy-done.4 = f32[2,16,128]{2,1,0:T(8,128)} copy-done((f32[2,16,128]{2,1,0:T(8,128)}, f32[2,16,128]{2,1,0:T(8,128)S(1)}, u32[]{:S(2)}) %copy-start.4) | copy-done | bytes 16408
  49.5 0.0 copy-start.5
  49.5 0.6 %copy-done.5 = f32[16,64]{1,0:T(8,128)} copy-done((f32[16,64]{1,0:T(8,128)}, f32[16,64]{1,0:T(8,128)S(1)}, u32[]{:S(2)}) %copy-start.5) | copy-done | bytes 4120
  50.1 1.9 %shard_map.137 = (bf16[128,512]{1,0:T(8,128)(2,1)}, bf16[128,512]{1,0:T(8,128)(2,1)}, bf16[128,512]{1,0:T(8,128)(2,1)}, bf16[128,512]{1,0:T(8,128)(2,1)}, f32[2,16,128]{2,1,0:T(8,128)}, /*index=5*/f32[16,64]{1,0:T(8,128)}) custom-call(bf16[128,512]{1,0:T(8,128)(2,1)} %copy-done, bf16[128,512]{1,0:T(8,128)(2,1)} %copy-done.1, bf16[128,512]{1,0:T(8,128)(2,1)} %copy-done.2, ...), custom_call_target="tpu_custom_call" | custom-call | tf_op jit(solution)/shard_map/pallas_call | solution.py:541
Async XLA Ops:
  46.3 0.7 %copy-start = (bf16[128,512]{1,0:T(8,128)(2,1)}, bf16[128,512]{1,0:T(8,128)(2,1)S(1)}, u32[]{:S(2)}) copy-start(bf16[128,512]{1,0:T(8,128)(2,1)S(1)} %get-tuple-element.18.refs_0_) | copy-start | bytes 393220
  47.0 0.7 %copy-start.1 = (bf16[128,512]{1,0:T(8,128)(2,1)}, bf16[128,512]{1,0:T(8,128)(2,1)S(1)}, u32[]{:S(2)}) copy-start(bf16[128,512]{1,0:T(8,128)(2,1)S(1)} %get-tuple-element.19.refs_1_) | copy-start | bytes 393220
  47.6 0.7 %copy-start.2 = (bf16[128,512]{1,0:T(8,128)(2,1)}, bf16[128,512]{1,0:T(8,128)(2,1)S(1)}, u32[]{:S(2)}) copy-start(bf16[128,512]{1,0:T(8,128)(2,1)S(1)} %get-tuple-element.20.refs_2_) | copy-start | bytes 393220
  48.3 0.7 %copy-start.3 = (bf16[128,512]{1,0:T(8,128)(2,1)}, bf16[128,512]{1,0:T(8,128)(2,1)S(1)}, u32[]{:S(2)}) copy-start(bf16[128,512]{1,0:T(8,128)(2,1)S(1)} %get-tuple-element.21.refs_3_) | copy-start | bytes 393220
  48.9 0.6 %copy-start.4 = (f32[2,16,128]{2,1,0:T(8,128)}, f32[2,16,128]{2,1,0:T(8,128)S(1)}, u32[]{:S(2)}) copy-start(f32[2,16,128]{2,1,0:T(8,128)S(1)} %get-tuple-element.22.refs_4_) | copy-start | bytes 49156
  49.5 0.6 %copy-start.5 = (f32[16,64]{1,0:T(8,128)}, f32[16,64]{1,0:T(8,128)S(1)}, u32[]{:S(2)}) copy-start(f32[16,64]{1,0:T(8,128)S(1)} %get-tuple-element.23.refs_5_) | copy-start | bytes 12292

commit v3 on v2

--- a/solution.py
+++ b/solution.py
@@ -19,6 +19,10 @@
 BINS = 256
 CHUNK = 16
 UNROLL = 8
+PLANE = sorted(
+    ((dy, dx) for dy in range(4) for dx in range(4) if dy or dx),
+    key=lambda d: -sum(min(step, 4 - step) for step in d),
+)
 
 
 def tables():
@@ -57,7 +61,7 @@
     w_part, w_pair, w_sum, w_plane, w_tiles, w_ring,
     f_part, f_pair, f_sum, f_plane, f_send, f_recv, f_turned,
     in_sem, z_send, z_recv, pair_send, pair_recv, plane_send, plane_recv,
-    ring_send, ring_recv, own_send, own_recv,
+    last_send, last_recv, own_send, own_recv,
 ):
     doc = lax.axis_index("dp")
     pos = lax.axis_index("ctx")
@@ -108,8 +112,8 @@
         return pltpu.make_async_remote_copy(
             src_ref=sbuf.at[slot, to],
             dst_ref=rbuf.at[slot, at],
-            send_sem=z_send.at[slot, to],
-            recv_sem=z_recv.at[slot, at],
+            send_sem=z_send.at[slot],
+            recv_sem=z_recv.at[slot],
             device_id=(doc, to),
             device_id_type=MESH,
         )
@@ -118,10 +122,19 @@
         for o in (4, 3, 5, 2, 6, 1, 7):
             ring_copy(slot, lax.rem(pos + o, CTX), pos).start()
 
+    def ring_all(slot):
+        most = pl.ds(0, CTX - 1)
+        return pltpu.make_async_remote_copy(
+            src_ref=sbuf.at[slot, most],
+            dst_ref=rbuf.at[slot, most],
+            send_sem=z_send.at[slot],
+            recv_sem=z_recv.at[slot],
+            device_id=(doc, lax.rem(pos + 1, CTX)),
+            device_id_type=MESH,
+        )
+
     def ring_wait(slot):
-        for o in (1, 7, 2, 6, 3, 5, 4):
-            src = lax.rem(pos + o, CTX)
-            ring_copy(slot, src, src).wait_recv()
+        ring_all(slot).wait_recv()
 
     def rows_tile(ref):
         return lambda h, p: ref[64 * h : 64 * h + 64, 128 * p : 128 * p + 128].astype(F32)
@@ -309,24 +322,30 @@
             device_id_type=MESH,
         )
 
-    def plane_copy(index, src, dst, to, at):
+    def plane_start(index, src, dst):
+        row, col = lax.div(chip, 4), lax.rem(chip, 4)
+        for dy, dx in PLANE:
+            to = 4 * lax.rem(row + dy, 4) + lax.rem(col + dx, 4)
+            pltpu.make_async_remote_copy(
+                src_ref=src.at[to],
+                dst_ref=dst.at[chip],
+                send_sem=plane_send.at[index],
+                recv_sem=plane_recv.at[index],
+                device_id=(2 * to + core, pos),
+                device_id_type=MESH,
+            ).start()
+        dst[chip] = src[chip]
+
+    def plane_all(index, src, dst):
+        most = pl.ds(0, CHIPS - 1)
         return pltpu.make_async_remote_copy(
-            src_ref=src.at[to],
-            dst_ref=dst.at[at],
-            send_sem=plane_send.at[index, to],
-            recv_sem=plane_recv.at[index, at],
-            device_id=(2 * to + core, pos),
+            src_ref=src.at[most],
+            dst_ref=dst.at[most],
+            send_sem=plane_send.at[index],
+            recv_sem=plane_recv.at[index],
+            device_id=(2 * lax.rem(chip + 1, CHIPS) + core, pos),
             device_id_type=MESH,
         )
-
-    def plane_start(index, src, dst):
-        for o in range(1, CHIPS):
-            plane_copy(index, src, dst, lax.rem(chip + o, CHIPS), chip).start()
-
-    def plane_wait(index, src, dst):
-        for o in range(1, CHIPS):
-            at = lax.rem(chip + o, CHIPS)
-            plane_copy(index, src, dst, at, at).wait_recv()
 
     correlate(v_spec, f_spec, True, 0)
     correlate(m_spec, s_spec, True, 1)
@@ -365,112 +384,120 @@
     f_pair_copy.wait_recv()
     f_sum[...] = (f_part[core].astype(F32) + f_pair[...].astype(F32)).astype(BF16)
     plane_start(0, f_sum, f_plane)
-    f_plane[chip] = f_sum[chip]
     correlate(g_first, f_spec, False)
     pack_blocks(5, split_tiles(inverse()))
     ring_start(5)
     w_pair_copy.wait_recv()
     w_sum[...] = (w_part[core].astype(F32) + w_pair[...].astype(F32)).astype(BF16)
     plane_start(1, w_sum, w_plane)
-    w_plane[chip] = w_sum[chip]
-    mixed[...] = jnp.dot(gated, weight[...], preferred_element_type=F32).astype(BF16)
-
-    for slot, out in ((4, grad_gate_one), (5, grad_value)):
+
+    def deliver(slot, out):
         ring_wait(slot)
         for p in range(4):
             for half, part in enumerate(row_tile(slot, p)):
                 out[64 * half : 64 * half + 64, 128 * p : 128 * p + 128] = part.astype(BF16)
 
+    deliver(4, grad_gate_one)
+    mixed[...] = jnp.dot(gated, weight[...], preferred_element_type=F32).astype(BF16)
+
     scale = 1.0 / 32
 
-    plane_wait(0, f_sum, f_plane)
-    f_send[...] = jnp.sum(f_plane[...].astype(F32), axis=0) * scale
+    plane_all(0, f_sum, f_plane).wait_recv()
+    total = jnp.sum(f_plane[...].astype(F32), axis=0) * scale
+    for k, part in enumerate(mix(total[:16], total[16:])):
+        f_send[k] = part.astype(BF16)
     piece_h = lax.div(doc, 16)
     piece_t = lax.rem(lax.div(doc, 8), 2)
     piece_g = lax.rem(doc, 8)
-
-    def owner(i):
-        return 4 * pos + i % 4, 2 * (2 * piece_t + i // 4) + piece_h
-
-    def own_copy(i, at):
-        to_doc, to_pos = owner(i)
+    first_doc = 16 * lax.rem(pos, 2) + 8 * lax.div(pos, 4)
+    owns_piece = jnp.logical_and(lax.div(doc, 4) == pos, first_doc + piece_g == doc)
+
+    for i in range(8):
+        to_doc, to_pos = 4 * pos + i % 4, 2 * (2 * piece_t + i // 4) + piece_h
+        is_self = jnp.logical_and(to_doc == doc, to_pos == pos)
+
+        @pl.when(jnp.logical_not(is_self))
+        def _():
+            pltpu.make_async_remote_copy(
+                src_ref=f_send.at[i // 4],
+                dst_ref=f_recv.at[piece_g],
+                send_sem=own_send,
+                recv_sem=own_recv,
+                device_id=(to_doc, to_pos),
+                device_id_type=MESH,
+            ).start()
+
+        @pl.when(is_self)
+        def _():
+            f_recv[piece_g] = f_send[i // 4]
+
+    def own_all(count):
         return pltpu.make_async_remote_copy(
-            src_ref=f_send,
-            dst_ref=f_recv.at[at],
-            send_sem=own_send.at[i],
-            recv_sem=own_recv.at[at],
-            device_id=(to_doc, to_pos),
+            src_ref=f_recv.at[pl.ds(0, count)],
+            dst_ref=f_recv.at[pl.ds(0, count)],
+            send_sem=own_send,
+            recv_sem=own_recv,
+            device_id=(doc, lax.rem(pos + 1, CTX)),
             device_id_type=MESH,
         )
 
-    def is_self(i):
-        to_doc, to_pos = owner(i)
-        return jnp.logical_and(to_doc == doc, to_pos == pos)
-
-    for i in range(8):
-
-        @pl.when(jnp.logical_not(is_self(i)))
-        def _():
-            own_copy(i, piece_g).start()
-
-        @pl.when(is_self(i))
-        def _():
-            f_recv[piece_g] = f_send[...]
-
-    def tile_copy(to, at):
-        return pltpu.make_async_remote_copy(
-            src_ref=w_tiles.at[lax.div(to, 2)],
-            dst_ref=w_ring.at[at],
-            send_sem=ring_send.at[to],
-            recv_sem=ring_recv.at[at],
-            device_id=(doc, to),
-            device_id_type=MESH,
-        )
-
-    plane_wait(1, w_sum, w_plane)
+    plane_all(1, w_sum, w_plane).wait_recv()
     w_total = jnp.sum(w_plane[...].astype(F32), axis=0).astype(BF16)
     for p in range(4):
         w_tiles[p] = w_total[:, 128 * p : 128 * p + 128]
     for o in (4, 3, 5, 2, 6, 1, 7):
-        tile_copy(lax.rem(pos + o, CTX), pos).start()
+        to = lax.rem(pos + o, CTX)
+        pltpu.make_async_remote_copy(
+            src_ref=w_tiles.at[lax.div(to, 2)],
+            dst_ref=w_ring.at[pos],
+            send_sem=last_send,
+            recv_sem=last_recv,
+            device_id=(doc, to),
+            device_id_type=MESH,
+        ).start()
     w_ring[pos] = w_tiles[lax.div(pos, 2)]
-    for o in range(1, CTX):
-        src = lax.rem(pos + o, CTX)
-        tile_copy(src, src).wait_recv()
+    last_all = pltpu.make_async_remote_copy(
+        src_ref=w_ring.at[pl.ds(0, CTX - 1)],
+        dst_ref=w_ring.at[pl.ds(0, CTX - 1)],
+        send_sem=last_send,
+        recv_sem=last_recv,
+        device_id=(doc, lax.rem(pos + 1, CTX)),
+        device_id_type=MESH,
+    )
+    deliver(5, grad_value)
+
+    @pl.when(owns_piece)
+    def _():
+        own_all(7).wait_recv()
+
+    @pl.when(jnp.logical_not(owns_piece))
+    def _():
+        own_all(8).wait_recv()
+
+    f_turned[...] = f_recv[...].astype(F32).reshape(ROWS, 128).T
+    for which in range(2):
+        first = pl.multiple_of(64 * which + 16 * lax.rem(doc, 4), 16)
+        filter_grad[which] = f_turned[pl.ds(first, 16), :]
+
+    last_all.wait_recv()
     total = jnp.sum(w_ring[...].astype(F32), axis=0) * scale
     weight_grad[...] = jnp.where(odd, turn(total), total)[:, :64]
 
-    from_pos = lax.div(doc, 4)
-    first_doc = 16 * lax.rem(pos, 2) + 8 * lax.div(pos, 4)
-    for g in range(8):
-
-        @pl.when(jnp.logical_not(jnp.logical_and(from_pos == pos, first_doc + g == doc)))
-        def _():
-            own_copy(0, g).wait_recv()
-
-    group = 4 * lax.rem(lax.div(pos, 2), 2) + lax.rem(doc, 4)
-    for which in range(2):
-        rows = f_recv[:, 16 * which : 16 * which + 16, :].reshape(ROWS, 128)
-        f_turned[which] = rows.T
-    for which in range(2):
-        filter_grad[which] = f_turned[which, pl.ds(pl.multiple_of(16 * group, 16), 16), :]
-
     for slot in range(6):
-        for o in range(1, CTX):
-            ring_copy(slot, lax.rem(pos + o, CTX), pos).wait_send()
+        ring_all(slot).wait_send()
     f_pair_copy.wait_send()
     w_pair_copy.wait_send()
-    for index, src, dst in ((0, f_sum, f_plane), (1, w_sum, w_plane)):
-        for o in range(1, CHIPS):
-            plane_copy(index, src, dst, lax.rem(chip + o, CHIPS), chip).wait_send()
-    for o in range(1, CTX):
-        tile_copy(lax.rem(pos + o, CTX), pos).wait_send()
-
-    for i in range(8):
-
-        @pl.when(jnp.logical_not(is_self(i)))
-        def _():
-            own_copy(i, piece_g).wait_send()
+    plane_all(0, f_sum, f_plane).wait_send()
+    plane_all(1, w_sum, w_plane).wait_send()
+    last_all.wait_send()
+
+    @pl.when(owns_piece)
+    def _():
+        own_all(7).wait_send()
+
+    @pl.when(jnp.logical_not(owns_piece))
+    def _():
+        own_all(8).wait_send()
 
 
 def finish(*refs):
@@ -518,20 +545,20 @@
             pltpu.VMEM((CHIPS, 32, 128), BF16),
             pltpu.VMEM((CHIPS, 32, 128), BF16),
             pltpu.VMEM((CHIPS, 32, 128), BF16),
-            pltpu.VMEM((32, 128), F32),
-            pltpu.VMEM((8, 32, 128), F32),
-            pltpu.VMEM((2, ROWS, 128), F32),
+            pltpu.VMEM((2, 16, 128), BF16),
+            pltpu.VMEM((8, 16, 128), BF16),
+            pltpu.VMEM((128, ROWS), F32),
             dma((9,)),
-            dma((6, CTX)),
-            dma((6, CTX)),
+            dma((6,)),
+            dma((6,)),
             dma((2,)),
             dma((2,)),
-            dma((2, CHIPS)),
-            dma((2, CHIPS)),
-            dma((CTX,)),
-            dma((CTX,)),
-            dma((8,)),
-            dma((8,)),
+            dma((2,)),
+            dma((2,)),
+            dma,
+            dma,
+            dma,
+            dma,
         ],
         compiler_params=pltpu.CompilerParams(collective_id=0, has_side_effects=True),
     )(
@@ -544,6 +571,7 @@
         in_specs=[vmem] * 6,
         out_specs=[anywhere] * 6,
         scratch_shapes=[dma((6,))],
+        compiler_params=pltpu.CompilerParams(vmem_limit_bytes=1 << 20),
     )(*outs)
     mixed, grad_value, grad_gate_one, grad_gate_two, filter_grad, weight_grad = outs
     return (

time: 52.2 us -> 40.4 us (0.77)
  Pallas kernels: 47.6 us -> 39.7 us
  local copies, waits for them, and re-layouts: 3.79 us -> 0 us
    pallas_call x1, Pallas kernels: 45.7 us -> 38.8 us  [on_device(): pl.pallas_call(kernel, out_shape=tuple((pltpu.VMEM(*shape) for shape in s...]
    unnamed x12 -> x0, local copies, waits for them, and re-layouts: 3.79 us -> none
    pallas_call x1, Pallas kernels: 1.94 us -> 0.84 us  [on_device(): pl.pallas_call(finish, out_shape=tuple((jax.ShapeDtypeStruct(*shape) for...]
where the time goes in v3:
time: 40.4 us; the launch traced here: 40.3 us
  Pallas kernels  39.7 us (98%)
  between operations  0.64 us (2%)
    pallas_call x1, Pallas kernels, on_device(): pl.pallas_call(kernel, out_shape=tuple((pltpu.VMEM(*shape) for shape in s...  38.8 us
    pallas_call x1, Pallas kernels, on_device(): pl.pallas_call(finish, out_shape=tuple((jax.ShapeDtypeStruct(*shape) for...  0.84 us

profile of v3, /device:TPU:1, one launch (start us, length us, event | category | flops | bytes accessed | tf_op | source)
XLA Modules:
  0.0 40.3 jit_solution(9055499422059213216)
XLA Ops:
  0.6 38.8 %shard_map.136 = (bf16[128,512]{1,0:T(8,128)(2,1)S(1)}, bf16[128,512]{1,0:T(8,128)(2,1)S(1)}, bf16[128,512]{1,0:T(8,128)(2,1)S(1)}, bf16[128,512]{1,0:T(8,128)(2...) custom-call(bf16[128,512]{1,0:T(8,128)(2,1)} %bitcast.9, bf16[128,512]{1,0:T(8,128)(2,1)} %bitcast.10, ...), custom_call_target="tpu_custom_call" | custom-call | tf_op jit(solution)/shard_map/pallas_call | solution.py:520
  39.5 0.8 %shard_map.137 = (bf16[128,512]{1,0:T(8,128)(2,1)}, bf16[128,512]{1,0:T(8,128)(2,1)}, bf16[128,512]{1,0:T(8,128)(2,1)}, bf16[128,512]{1,0:T(8,128)(2,1)}, f32[2,16,128]{2,1,0:T(8,128)}, /*index=5*/f32[16,64]{1,0:T(8,128)}) custom-call(bf16[128,512]{1,0:T(8,128)(2,1)S(1)} %get-tuple-element.18.refs_0_, bf16[128,512]{1,0:T(8,128)(2,1)S(1)} %get-tuple-element.19.refs_1_, ...), custom_call_target="tpu_custom_call" | custom-call | tf_op jit(solution)/shard_map/pallas_call | solution.py:568

commit v4 on v3

--- a/solution.py
+++ b/solution.py
@@ -185,14 +185,14 @@
     def plus(*terms):
         return sum(t[0] for t in terms[1:]) + terms[0][0], sum(t[1] for t in terms[1:]) + terms[0][1]
 
-    def chunks(body):
+    def chunks(body, unroll=UNROLL):
         for half, sign in ((0, 1.0), (1, -1.0)):
 
             def step(i, carry):
                 body(pl.multiple_of(half * (BINS // 2) + i * CHUNK, CHUNK), sign)
                 return carry
 
-            lax.fori_loop(0, BINS // 2 // CHUNK, step, 0, unroll=UNROLL)
+            lax.fori_loop(0, BINS // 2 // CHUNK, step, 0, unroll=unroll)
 
     def spread(g01, g23):
         t01, t23 = both(g01), both(g23)
@@ -229,7 +229,7 @@
             out23 = plus(conj_times(h0, y23), conj_times(low_only(t01), y32))
             store(slot, r, out01, out23)
 
-        chunks(body)
+        chunks(body, UNROLL // 2 if windows else UNROLL)
 
     odd = lax.rem(pos, 2) == 1
 
@@ -308,7 +308,6 @@
     correlate(g_second, s_spec, False)
     grad_mixed = inverse()
     pack_blocks(4, split_tiles(grad_mixed * first_conv[...]))
-    ring_start(4)
     to_columns(1, grad_mixed)
     forward(f_spec)
 
@@ -322,19 +321,26 @@
             device_id_type=MESH,
         )
 
-    def plane_start(index, src, dst):
-        row, col = lax.div(chip, 4), lax.rem(chip, 4)
+    row, col = lax.div(chip, 4), lax.rem(chip, 4)
+
+    def piece_of(y, x):
+        dy = lax.rem(y + 4 - lax.div(pos, 2), 4)
+        dx = lax.rem(x + 4 - 2 * lax.rem(pos, 2), 4)
+        away = jnp.where(dx >= 2, lax.rem(10 - dy, 8), 3 + lax.rem(dy + 1, 4))
+        return 2 * lax.rem(pos + away, CTX) + lax.rem(dx, 2)
+
+    def plane_start(index, src, dst, slot_of):
         for dy, dx in PLANE:
-            to = 4 * lax.rem(row + dy, 4) + lax.rem(col + dx, 4)
+            y, x = lax.rem(row + dy, 4), lax.rem(col + dx, 4)
             pltpu.make_async_remote_copy(
-                src_ref=src.at[to],
+                src_ref=src.at[slot_of(y, x)],
                 dst_ref=dst.at[chip],
                 send_sem=plane_send.at[index],
                 recv_sem=plane_recv.at[index],
-                device_id=(2 * to + core, pos),
+                device_id=(2 * (4 * y + x) + core, pos),
                 device_id_type=MESH,
             ).start()
-        dst[chip] = src[chip]
+        dst[chip] = src[slot_of(row, col)]
 
     def plane_all(index, src, dst):
         most = pl.ds(0, CHIPS - 1)
@@ -349,18 +355,18 @@
 
     correlate(v_spec, f_spec, True, 0)
     correlate(m_spec, s_spec, True, 1)
-    for which in range(2):
-        lags = inverse(which).astype(BF16)
-        for h in range(2):
-            for t in range(2):
-                for g in range(8):
-                    row = 128 * h + 16 * g
-                    f_part[g % 2, 4 * (2 * h + t) + g // 2, 16 * which : 16 * which + 16, :] = lags[
-                        row : row + 16, 128 * t : 128 * t + 128
-                    ]
+    lags = [inverse(which) for which in range(2)]
+    for h in range(2):
+        for t in range(2):
+            where = (slice(128 * h, 128 * h + 128), slice(128 * t, 128 * t + 128))
+            for k, part in enumerate(mix(lags[0][where], lags[1][where])):
+                part = part.astype(BF16)
+                for rho in range(4):
+                    piece = 2 * (2 * (2 * t + k) + h) + rho // 2
+                    f_part[rho % 2, piece] = part[32 * rho : 32 * rho + 32]
     f_pair_copy = pair_copy(0, f_part, f_pair)
     f_pair_copy.start()
-
+    ring_start(4)
     def row_tile(slot, p):
         return mix(rbuf[slot, 2 * p].astype(F32), rbuf[slot, 2 * p + 1].astype(F32))
 
@@ -377,19 +383,19 @@
             gated_t[128 * c : 128 * c + 128], grad_out[...], preferred_element_type=F32
         ).astype(BF16)
         for i in range(8):
-            row = 16 * (4 * c + i // 2)
             w_part[i % 2, 4 * c + i // 2] = part[16 * i : 16 * i + 16]
     w_pair_copy = pair_copy(1, w_part, w_pair)
     w_pair_copy.start()
-    f_pair_copy.wait_recv()
-    f_sum[...] = (f_part[core].astype(F32) + f_pair[...].astype(F32)).astype(BF16)
-    plane_start(0, f_sum, f_plane)
     correlate(g_first, f_spec, False)
     pack_blocks(5, split_tiles(inverse()))
     ring_start(5)
+    f_pair_copy.wait_recv()
+    f_sum[...] = (f_part[core].astype(F32) + f_pair[...].astype(F32)).astype(BF16)
+    plane_start(0, f_sum, f_plane, piece_of)
+
     w_pair_copy.wait_recv()
     w_sum[...] = (w_part[core].astype(F32) + w_pair[...].astype(F32)).astype(BF16)
-    plane_start(1, w_sum, w_plane)
+    plane_start(1, w_sum, w_plane, lambda y, x: 4 * y + x)
 
     def deliver(slot, out):
         ring_wait(slot)
@@ -397,49 +403,32 @@
             for half, part in enumerate(row_tile(slot, p)):
                 out[64 * half : 64 * half + 64, 128 * p : 128 * p + 128] = part.astype(BF16)
 
-    deliver(4, grad_gate_one)
-    mixed[...] = jnp.dot(gated, weight[...], preferred_element_type=F32).astype(BF16)
-
     scale = 1.0 / 32
 
     plane_all(0, f_sum, f_plane).wait_recv()
     total = jnp.sum(f_plane[...].astype(F32), axis=0) * scale
-    for k, part in enumerate(mix(total[:16], total[16:])):
-        f_send[k] = part.astype(BF16)
-    piece_h = lax.div(doc, 16)
-    piece_t = lax.rem(lax.div(doc, 8), 2)
-    piece_g = lax.rem(doc, 8)
-    first_doc = 16 * lax.rem(pos, 2) + 8 * lax.div(pos, 4)
-    owns_piece = jnp.logical_and(lax.div(doc, 4) == pos, first_doc + piece_g == doc)
-
-    for i in range(8):
-        to_doc, to_pos = 4 * pos + i % 4, 2 * (2 * piece_t + i // 4) + piece_h
-        is_self = jnp.logical_and(to_doc == doc, to_pos == pos)
-
-        @pl.when(jnp.logical_not(is_self))
-        def _():
-            pltpu.make_async_remote_copy(
-                src_ref=f_send.at[i // 4],
-                dst_ref=f_recv.at[piece_g],
-                send_sem=own_send,
-                recv_sem=own_recv,
-                device_id=(to_doc, to_pos),
-                device_id_type=MESH,
-            ).start()
-
-        @pl.when(is_self)
-        def _():
-            f_recv[piece_g] = f_send[i // 4]
-
-    def own_all(count):
-        return pltpu.make_async_remote_copy(
-            src_ref=f_recv.at[pl.ds(0, count)],
-            dst_ref=f_recv.at[pl.ds(0, count)],
+    even = lax.rem(lax.div(lax.broadcasted_iota(jnp.int32, (16, 128), 1), 32), 2) == 0
+    f_send[0] = jnp.where(even, total[:16], turn(total[16:], 32)).astype(BF16)
+    f_send[1] = jnp.where(even, turn(total[:16], 96), total[16:]).astype(BF16)
+    piece = piece_of(row, col)
+    rho = 2 * lax.rem(piece, 2) + core
+    for q in range(4):
+        pltpu.make_async_remote_copy(
+            src_ref=f_send.at[q // 2],
+            dst_ref=f_recv.at[rho],
             send_sem=own_send,
             recv_sem=own_recv,
-            device_id=(doc, lax.rem(pos + 1, CTX)),
+            device_id=(4 * pos + q, lax.div(piece, 2)),
             device_id_type=MESH,
-        )
+        ).start()
+    own_all = pltpu.make_async_remote_copy(
+        src_ref=f_recv,
+        dst_ref=f_recv,
+        send_sem=own_send,
+        recv_sem=own_recv,
+        device_id=(doc, lax.rem(pos + 1, CTX)),
+        device_id_type=MESH,
+    )
 
     plane_all(1, w_sum, w_plane).wait_recv()
     w_total = jnp.sum(w_plane[...].astype(F32), axis=0).astype(BF16)
@@ -464,19 +453,18 @@
         device_id=(doc, lax.rem(pos + 1, CTX)),
         device_id_type=MESH,
     )
+    deliver(4, grad_gate_one)
     deliver(5, grad_value)
-
-    @pl.when(owns_piece)
-    def _():
-        own_all(7).wait_recv()
-
-    @pl.when(jnp.logical_not(owns_piece))
-    def _():
-        own_all(8).wait_recv()
-
-    f_turned[...] = f_recv[...].astype(F32).reshape(ROWS, 128).T
+    mixed[...] = jnp.dot(gated, weight[...], preferred_element_type=F32).astype(BF16)
+
+    own_all.wait_recv()
+    lags = []
+    for rho in range(4):
+        part = f_recv[rho].astype(F32)
+        lags += [part, turn(part, 96)]
+    f_turned[...] = jnp.concatenate(lags, axis=0).T
     for which in range(2):
-        first = pl.multiple_of(64 * which + 16 * lax.rem(doc, 4), 16)
+        first = pl.multiple_of(64 * which + 16 * core, 16)
         filter_grad[which] = f_turned[pl.ds(first, 16), :]
 
     last_all.wait_recv()
@@ -491,13 +479,7 @@
     plane_all(1, w_sum, w_plane).wait_send()
     last_all.wait_send()
 
-    @pl.when(owns_piece)
-    def _():
-        own_all(7).wait_send()
-
-    @pl.when(jnp.logical_not(owns_piece))
-    def _():
-        own_all(8).wait_send()
+    own_all.wait_send()
 
 
 def finish(*refs):
@@ -546,7 +528,7 @@
             pltpu.VMEM((CHIPS, 32, 128), BF16),
             pltpu.VMEM((CHIPS, 32, 128), BF16),
             pltpu.VMEM((2, 16, 128), BF16),
-            pltpu.VMEM((8, 16, 128), BF16),
+            pltpu.VMEM((4, 16, 128), BF16),
             pltpu.VMEM((128, ROWS), F32),
             dma((9,)),
             dma((6,)),

time: 40.4 us -> 39.3 us (0.973)
  Pallas kernels: 39.7 us -> 38.6 us
    pallas_call x1, Pallas kernels: 38.8 us -> 37.7 us  [on_device(): pl.pallas_call(kernel, out_shape=tuple((pltpu.VMEM(*shape) for shape in s...]
where the time goes in v4:
time: 39.3 us; the launch traced here: 39.2 us
  Pallas kernels  38.6 us (98%)
  between operations  0.64 us (2%)
    pallas_call x1, Pallas kernels, on_device(): pl.pallas_call(kernel, out_shape=tuple((pltpu.VMEM(*shape) for shape in s...  37.7 us
    pallas_call x1, Pallas kernels, on_device(): pl.pallas_call(finish, out_shape=tuple((jax.ShapeDtypeStruct(*shape) for...  0.84 us

profile of v4, /device:TPU:1, one launch (start us, length us, event | category | flops | bytes accessed | tf_op | source)
XLA Modules:
  0.0 39.2 jit_solution(11479146295571590024)
XLA Ops:
  0.6 37.7 %shard_map.136 = (bf16[128,512]{1,0:T(8,128)(2,1)S(1)}, bf16[128,512]{1,0:T(8,128)(2,1)S(1)}, bf16[128,512]{1,0:T(8,128)(2,1)S(1)}, bf16[128,512]{1,0:T(8,128)(2...) custom-call(bf16[128,512]{1,0:T(8,128)(2,1)} %bitcast.9, bf16[128,512]{1,0:T(8,128)(2,1)} %bitcast.10, ...), custom_call_target="tpu_custom_call" | custom-call | tf_op jit(solution)/shard_map/pallas_call | solution.py:502
  38.4 0.8 %shard_map.137 = (bf16[128,512]{1,0:T(8,128)(2,1)}, bf16[128,512]{1,0:T(8,128)(2,1)}, bf16[128,512]{1,0:T(8,128)(2,1)}, bf16[128,512]{1,0:T(8,128)(2,1)}, f32[2,16,128]{2,1,0:T(8,128)}, /*index=5*/f32[16,64]{1,0:T(8,128)}) custom-call(bf16[128,512]{1,0:T(8,128)(2,1)S(1)} %get-tuple-element.18.refs_0_, bf16[128,512]{1,0:T(8,128)(2,1)S(1)} %get-tuple-element.19.refs_1_, ...), custom_call_target="tpu_custom_call" | custom-call | tf_op jit(solution)/shard_map/pallas_call | solution.py:550

commit v5 on v4

--- a/solution.py
+++ b/solution.py
@@ -56,7 +56,7 @@
     value_hbm, gate_one_hbm, gate_two_hbm, grad_out_hbm, filters_hbm, weight_hbm, fh_hbm, fl_hbm, ih_hbm,
     mixed, grad_value, grad_gate_one, grad_gate_two, filter_grad, weight_grad,
     value, gate_one, gate_two, grad_out, weight, fh, fl, ih, filt,
-    sbuf, rbuf, g_first, g_second, v_spec, m_spec, s_spec, f_spec, product,
+    sbuf, rbuf, g_first, g_second, v_spec, m_spec, s_spec, f_spec, forms, product,
     first_conv, grad_gated, xt,
     w_part, w_pair, w_sum, w_plane, w_tiles, w_ring,
     f_part, f_pair, f_sum, f_plane, f_send, f_recv, f_turned,
@@ -69,12 +69,13 @@
     chip = lax.div(doc, 2)
 
     barrier = pltpu.get_barrier_semaphore()
-    for o in range(1, CTX):
+    row, col = lax.div(chip, 4), lax.rem(chip, 4)
+    for o in (4, 3, 5, 2, 6, 1, 7):
         pl.semaphore_signal(barrier, inc=1, device_id=(doc, lax.rem(pos + o, CTX)), device_id_type=MESH)
+    for dy, dx in PLANE:
+        peer = 2 * (4 * lax.rem(row + dy, 4) + lax.rem(col + dx, 4)) + core
+        pl.semaphore_signal(barrier, inc=1, device_id=(peer, pos), device_id_type=MESH)
     pl.semaphore_signal(barrier, inc=1, device_id=(2 * chip + 1 - core, pos), device_id_type=MESH)
-    for o in range(1, CHIPS):
-        peer = 2 * lax.rem(chip + o, CHIPS) + core
-        pl.semaphore_signal(barrier, inc=1, device_id=(peer, pos), device_id_type=MESH)
 
     column = pl.multiple_of(lax.div(pos, 2) * 128, 128)
     loads = {}
@@ -211,25 +212,46 @@
 
         chunks(body)
 
-    def correlate(filter_spec, data_spec, windows, slot=0):
+    def forms_of(spec):
+        def at(r):
+            h0, h1, h2, t01, t23 = spread(*load(spec, r))
+            return h0, h1, h2, low_only(t23), low_only(t01)
+
+        return at
+
+    def prepare(index, spec):
         def body(r, sign):
-            g01, g23 = load(filter_spec, r)
+            for n, form in enumerate(forms_of(spec)(r)):
+                for part in range(2):
+                    forms[index, n, pl.ds(part * BINS + r, CHUNK), :] = form[part]
+
+        chunks(body)
+
+        def at(r):
+            return tuple(
+                tuple(forms[index, n, pl.ds(part * BINS + r, CHUNK), :] for part in range(2)) for n in range(5)
+            )
+
+        return at
+
+    def correlate(filter_forms, data_spec, windows, slot=0):
+        def body(r, sign):
             y01, y23 = load(data_spec, r)
             if windows:
                 t01, t23 = both(y01), both(y23)
                 n01, n23 = pick(t01, t23), low_only(t23)
                 y01 = (y01[0] + sign * n01[1], y01[1] - sign * n01[0])
                 y23 = (y23[0] + sign * n23[1], y23[1] - sign * n23[0])
-            h0, h1, h2, t01, t23 = spread(g01, g23)
+            h0, h1, h2, low3, low1 = filter_forms(r)
             y10, y32 = both(y01), both(y23)
             y12 = pick(y10, y32)
             out01 = plus(
-                conj_times(h0, y01), conj_times(h1, y12), conj_times(h2, y23), conj_times(low_only(t23), y32)
+                conj_times(h0, y01), conj_times(h1, y12), conj_times(h2, y23), conj_times(low3, y32)
             )
-            out23 = plus(conj_times(h0, y23), conj_times(low_only(t01), y32))
+            out23 = plus(conj_times(h0, y23), conj_times(low1, y32))
             store(slot, r, out01, out23)
 
-        chunks(body, UNROLL // 2 if windows else UNROLL)
+        chunks(body, UNROLL)
 
     odd = lax.rem(pos, 2) == 1
 
@@ -290,11 +312,13 @@
     def split_tiles(x):
         return x[:, :128], x[:, 128:]
 
+    second_forms = prepare(0, g_second)
     ring_wait(0)
     to_columns(0)
     forward(v_spec)
     convolve(g_first, v_spec)
     first_conv[...] = inverse()
+    value_forms = prepare(1, v_spec)
     ring_wait(1)
     to_columns(1, first_conv)
     forward(m_spec)
@@ -302,12 +326,12 @@
     pack_blocks(3, split_tiles(inverse()))
     ring_start(3)
 
+    mixed_forms = prepare(2, m_spec)
     ring_wait(2)
     to_columns(2)
     forward(s_spec)
-    correlate(g_second, s_spec, False)
+    correlate(second_forms, s_spec, False)
     grad_mixed = inverse()
-    pack_blocks(4, split_tiles(grad_mixed * first_conv[...]))
     to_columns(1, grad_mixed)
     forward(f_spec)
 
@@ -320,8 +344,6 @@
             device_id=(2 * chip + 1 - core, pos),
             device_id_type=MESH,
         )
-
-    row, col = lax.div(chip, 4), lax.rem(chip, 4)
 
     def piece_of(y, x):
         dy = lax.rem(y + 4 - lax.div(pos, 2), 4)
@@ -353,8 +375,8 @@
             device_id_type=MESH,
         )
 
-    correlate(v_spec, f_spec, True, 0)
-    correlate(m_spec, s_spec, True, 1)
+    correlate(value_forms, f_spec, True, 0)
+    correlate(mixed_forms, s_spec, True, 1)
     lags = [inverse(which) for which in range(2)]
     for h in range(2):
         for t in range(2):
@@ -366,6 +388,7 @@
                     f_part[rho % 2, piece] = part[32 * rho : 32 * rho + 32]
     f_pair_copy = pair_copy(0, f_part, f_pair)
     f_pair_copy.start()
+    pack_blocks(4, split_tiles(grad_mixed * first_conv[...]))
     ring_start(4)
     def row_tile(slot, p):
         return mix(rbuf[slot, 2 * p].astype(F32), rbuf[slot, 2 * p + 1].astype(F32))
@@ -386,9 +409,6 @@
             w_part[i % 2, 4 * c + i // 2] = part[16 * i : 16 * i + 16]
     w_pair_copy = pair_copy(1, w_part, w_pair)
     w_pair_copy.start()
-    correlate(g_first, f_spec, False)
-    pack_blocks(5, split_tiles(inverse()))
-    ring_start(5)
     f_pair_copy.wait_recv()
     f_sum[...] = (f_part[core].astype(F32) + f_pair[...].astype(F32)).astype(BF16)
     plane_start(0, f_sum, f_plane, piece_of)
@@ -397,6 +417,9 @@
     w_sum[...] = (w_part[core].astype(F32) + w_pair[...].astype(F32)).astype(BF16)
     plane_start(1, w_sum, w_plane, lambda y, x: 4 * y + x)
 
+    correlate(forms_of(g_first), f_spec, False)
+    pack_blocks(5, split_tiles(inverse()))
+    ring_start(5)
     def deliver(slot, out):
         ring_wait(slot)
         for p in range(4):
@@ -513,6 +536,7 @@
             pltpu.VMEM((6, CTX, 64, 128), BF16),
             pltpu.VMEM((6, CTX, 64, 128), BF16),
             spectrum, spectrum, spectrum, spectrum, spectrum, spectrum,
+            pltpu.VMEM((3, 5, 2 * BINS, 128), F32),
             pltpu.VMEM((2, 2 * BINS, 256), BF16),
             pltpu.VMEM((BLK, 256), F32),
             pltpu.VMEM((ROWS, WIDTH), F32),

time: 39.3 us -> 39.9 us (1.015)
  Pallas kernels: 38.6 us -> 39.1 us
    pallas_call x1, Pallas kernels: 37.7 us -> 38.3 us  [on_device(): pl.pallas_call(kernel, out_shape=tuple((pltpu.VMEM(*shape) for shape in s...]
where the time goes in v5:
time: 39.9 us; the launch traced here: 39.8 us
  Pallas kernels  39.1 us (98%)
  between operations  0.64 us (2%)
    pallas_call x1, Pallas kernels, on_device(): pl.pallas_call(kernel, out_shape=tuple((pltpu.VMEM(*shape) for shape in s...  38.3 us
    pallas_call x1, Pallas kernels, on_device(): pl.pallas_call(finish, out_shape=tuple((jax.ShapeDtypeStruct(*shape) for...  0.84 us

profile of v5, /device:TPU:1, one launch (start us, length us, event | category | flops | bytes accessed | tf_op | source)
XLA Modules:
  0.0 39.8 jit_solution(2971176202042406827)
XLA Ops:
  0.6 38.3 %shard_map.136 = (bf16[128,512]{1,0:T(8,128)(2,1)S(1)}, bf16[128,512]{1,0:T(8,128)(2,1)S(1)}, bf16[128,512]{1,0:T(8,128)(2,1)S(1)}, bf16[128,512]{1,0:T(8,128)(2...) custom-call(bf16[128,512]{1,0:T(8,128)(2,1)} %bitcast.9, bf16[128,512]{1,0:T(8,128)(2,1)} %bitcast.10, ...), custom_call_target="tpu_custom_call" | custom-call | tf_op jit(solution)/shard_map/pallas_call | solution.py:525
  38.9 0.8 %shard_map.137 = (bf16[128,512]{1,0:T(8,128)(2,1)}, bf16[128,512]{1,0:T(8,128)(2,1)}, bf16[128,512]{1,0:T(8,128)(2,1)}, bf16[128,512]{1,0:T(8,128)(2,1)}, f32[2,16,128]{2,1,0:T(8,128)}, /*index=5*/f32[16,64]{1,0:T(8,128)}) custom-call(bf16[128,512]{1,0:T(8,128)(2,1)S(1)} %get-tuple-element.18.refs_0_, bf16[128,512]{1,0:T(8,128)(2,1)S(1)} %get-tuple-element.19.refs_1_, ...), custom_call_target="tpu_custom_call" | custom-call | tf_op jit(solution)/shard_map/pallas_call | solution.py:574
